TPU v7x, 128 devices: a whole 4x4x4 slice. The times are simulated.
128 devices in a mesh: gx: 4 (over y), gy: 8 (over z, core), row: 4 (over x).
Axes of the slice: x: 4, y: 4, z: 4, core: 2. Of those that a mesh axis runs over, the one named last changes fastest.
Arguments:
- occupancy: int32 [32, 512, 4096], P('row', 'gx', 'gy'), may hold values 0 or 1
- random_draws: bfloat16 [4, 32, 512, 4096], P(None, 'row', 'gx', 'gy'), may hold values from 0 to 1
Outputs:
- coverage: float32 [128, 1024], P('gx', 'gy')
- projected: float32 [128, 1024], P('gx', 'gy')
All inputs are finite; a program needn't handle non-finite values. No bound on the sum of `occupancy` on one device may be relied on, other than what follows from the above.
Results may differ from a plain program's by a relative error of at most 0.0003.
Values may be sent and summed in bfloat16 or wider, within the bound.
A program may use at most 64 MiB of HBM per device.

v0:
```python
import jax
import jax.numpy as jnp
from jax import lax
from jax.sharding import PartitionSpec as P

SWEEPS = 4
BLOCK = 4
LEAP = 8


ADSORB = 0.6
DESORB = 0.6
HOPPING = 0.3
COUPLING = 0.5


def extended(shard, sides, width):
    edges = {}
    for axis, dim in sides:
        size, length = (lax.axis_size(axis), shard.shape[dim])
        up = [(i, (i + 1) % size) for i in range(size)]
        last = lax.slice_in_dim(shard, length - width, length, axis=dim)
        first = lax.slice_in_dim(shard, 0, width, axis=dim)
        edges[dim] = (
            lax.ppermute(last, axis, up),
            lax.ppermute(first, axis, [(b, a) for a, b in up]),
        )
    done = []
    for _, dim in sides:
        low, high = edges[dim]
        around = [(width, width) if d in done else (0, 0) for d in range(shard.ndim)]
        shard = jnp.concatenate([jnp.pad(low, around), shard, jnp.pad(high, around)], axis=dim)
        done.append(dim)
    return shard


def sent_to_all(shard, axis):
    copies = jnp.broadcast_to(shard, (lax.axis_size(axis), *shard.shape))
    return lax.all_to_all(copies, axis, split_axis=0, concat_axis=0, tiled=True)


def taken_together(shard, axis):
    everything = sent_to_all(shard, axis)
    return jnp.sum(everything, axis=0)


def sublattice_update(padded, jitter, colour):
    centre = padded[..., 1:-1, 1:-1]
    beside = (
        padded[..., 2:, 1:-1]
        + padded[..., :-2, 1:-1]
        + padded[..., 1:-1, 2:]
        + padded[..., 1:-1, :-2]
    )
    updated = (
        centre
        + ADSORB * jitter * (1.0 - centre)
        - DESORB * (1.0 - jitter) * jnp.exp(-COUPLING * beside) * centre
        + HOPPING * (0.25 * beside - centre)
    )
    row_index = lax.broadcasted_iota(jnp.int32, centre.shape[-2:], 0)
    col_index = lax.broadcasted_iota(jnp.int32, centre.shape[-2:], 1)
    chosen = (row_index + col_index + colour) % 2 == 0
    return jnp.where(chosen[None], updated, centre)


def block_sums(field):
    height, width = (field.shape[-2], field.shape[-1])
    shaped = field.reshape(field.shape[:-2] + (height // BLOCK, BLOCK, width // BLOCK, BLOCK))
    return jnp.sum(shaped, axis=(-3, -1))


def per_device(occupancy, random_draws):
    occupied = occupancy.astype(jnp.float32)
    earlier = occupied
    for sweep_index in range(SWEEPS):
        if sweep_index == SWEEPS - 2:
            earlier = occupied
        padded = extended(occupied, (("gx", 1), ("gy", 2)), 1)
        occupied = sublattice_update(
            padded, random_draws[sweep_index].astype(jnp.float32), sweep_index % 2
        )
    snapshots = jnp.stack([jnp.sum(earlier, axis=0), jnp.sum(occupied, axis=0)])
    coarse_sums = taken_together(block_sums(snapshots), "row")
    divisor = jnp.float32(occupancy.shape[0] * lax.axis_size("row") * BLOCK * BLOCK)
    averages = coarse_sums / divisor
    coverage = averages[1]
    projected = coverage + LEAP / 2.0 * (coverage - averages[0])
    return (coverage, projected)


def solution(mesh):
    in_specs = (P("row", "gx", "gy"), P(None, "row", "gx", "gy"))
    out_specs = (P("gx", "gy"), P("gx", "gy"))
    return jax.shard_map(
        per_device, mesh=mesh, in_specs=in_specs, out_specs=out_specs, check_vma=False
    )
```

profile of v0, /device:TPU:0, one launch (start us, length us, event | category | flops | bytes accessed | tf_op | source)
XLA Modules:
  0.0 104.3 jit_solution(10422503265767039409)
XLA Ops:
  0.6 2.0 %convert_element_type.28 = f32[8,128,512]{2,1,0:T(8,128)S(1)} convert(s32[8,128,512]{2,1,0:T(8,128)} %param.2) | non-fusion elementwise | flops 524288 | bytes 4194304 | tf_op jit(solution)/shard_map/convert_element_type | solution.py:74
  2.7 1.7 %collective-permute-start.1 = (f32[8,1,512]{2,1,0:T(1,128)S(1)}, f32[8,1,512]{2,1,0:T(1,128)S(1)}, u32[]{:S(2)}, u32[]{:S(2)}) collective-permute-start(f32[8,1,512]{2,1,0:T(1,128)S(1)} %get-tuple-element.20), channel_id=1, source_target_pairs={{0,32},{32,64},{64,96},{96,0},{1,33},{33,65},{65,97},{97,1},{2,34}... | collective-permute-start | bytes 49160 | tf_op jit(solution)/shard_map/ppermute | solution.py:25
  4.4 1.6 %collective-permute-start = (f32[8,1,512]{2,1,0:T(1,128)S(1)}, f32[8,1,512]{2,1,0:T(1,128)S(1)}, u32[]{:S(2)}, u32[]{:S(2)}) collective-permute-start(f32[8,1,512]{2,1,0:T(1,128)S(1)} %get-tuple-element.21), channel_id=1, source_target_pairs={{32,0},{64,32},{96,64},{0,96},{33,1},{65,33},{97,65},{1,97},{34,2}... | collective-permute-start | bytes 49160 | tf_op jit(solution)/shard_map/ppermute | solution.py:26
  6.2 3.2 %collective-permute-start.2 = (f32[8,128,1]{2,1,0:T(8,128)S(1)}, f32[8,128,1]{2,1,0:T(8,128)S(1)}, u32[]{:S(2)}, u32[]{:S(2)}) collective-permute-start(f32[8,128,1]{2,1,0:T(8,128)S(1)} %get-tuple-element.18), channel_id=1, source_target_pairs={{4,0},{8,4},{12,8},{16,12},{20,16},{24,20},{28,24},{0,28},{5,1},{9... | collective-permute-start | bytes 12296 | tf_op jit(solution)/shard_map/ppermute | solution.py:26
  9.4 6.6 %collective-permute-done.2 = f32[8,128,1]{2,1,0:T(8,128)S(1)} collective-permute-done((f32[8,128,1]{2,1,0:T(8,128)S(1)}, f32[8,128,1]{2,1,0:T(8,128)S(1)}, u32[]{:S(2)}, u32[]{:S(2)}) %collective-permute-start.2) | collective-permute-done | bytes 4128 | tf_op jit(solution)/shard_map/ppermute | solution.py:26
  16.1 3.1 %collective-permute-done.3 = f32[8,128,1]{2,1,0:T(8,128)S(1)} collective-permute-done((f32[8,128,1]{2,1,0:T(8,128)S(1)}, f32[8,128,1]{2,1,0:T(8,128)S(1)}, u32[]{:S(2)}, u32[]{:S(2)}) %collective-permute-start.3) | collective-permute-done | bytes 4128 | tf_op jit(solution)/shard_map/ppermute | solution.py:25
  19.2 2.7 %fusion.5 = f32[8,128,512]{2,1,0:T(8,128)S(1)} fusion(f32[8,128,512]{2,1,0:T(8,128)S(1)} %convert_element_type.28, f32[8,1,512]{2,1,0:T(1,128)S(1)} %collective-permute-done, f32[8,1,512]{2,1,0:T(1,128)S(1)} %collective-permute-done.1, f32[8,128,1]{2,1,0:T(8,128)S(1)} %collective-permute-done.3, f32[8,128,1]{2,1,0:T(8,128)S(1)} %collective-permute-done.2, ...), kind=kLoop, calls=%fused_computation.13 | loop fusion | flops 17301504 | bytes 5349376 | tf_op jit(solution)/shard_map/jit(_where)/select_n | solution.py:64
  22.4 3.0 %collective-permute-start.4 = (f32[8,1,512]{2,1,0:T(1,128)S(1)}, f32[8,1,512]{2,1,0:T(1,128)S(1)}, u32[]{:S(2)}, u32[]{:S(2)}) collective-permute-start(f32[8,1,512]{2,1,0:T(1,128)S(1)} %get-tuple-element.17), channel_id=1, source_target_pairs={{32,0},{64,32},{96,64},{0,96},{33,1},{65,33},{97,65},{1,97},{34,2}... | collective-permute-start | bytes 49160 | tf_op jit(solution)/shard_map/ppermute | solution.py:26
  26.0 6.1 %collective-permute-done.6 = f32[8,128,1]{2,1,0:T(8,128)S(1)} collective-permute-done((f32[8,128,1]{2,1,0:T(8,128)S(1)}, f32[8,128,1]{2,1,0:T(8,128)S(1)}, u32[]{:S(2)}, u32[]{:S(2)}) %collective-permute-start.6) | collective-permute-done | bytes 4128 | tf_op jit(solution)/shard_map/ppermute | solution.py:26
  32.1 3.1 %collective-permute-done.7 = f32[8,128,1]{2,1,0:T(8,128)S(1)} collective-permute-done((f32[8,128,1]{2,1,0:T(8,128)S(1)}, f32[8,128,1]{2,1,0:T(8,128)S(1)}, u32[]{:S(2)}, u32[]{:S(2)}) %collective-permute-start.7) | collective-permute-done | bytes 4128 | tf_op jit(solution)/shard_map/ppermute | solution.py:25
  35.2 2.7 %fusion.71 = (f32[128,512]{1,0:T(8,128)S(1)}, f32[8,128,512]{2,1,0:T(8,128)S(1)}) fusion(f32[8,128,512]{2,1,0:T(8,128)S(1)} %fusion.5, f32[8,1,512]{2,1,0:T(1,128)S(1)} %collective-permute-done.4, f32[8,1,512]{2,1,0:T(1,128)S(1)} %collective-permute-done.5, f32[8,128,1]{2,1,0:T(8,128)S(1)} %collective-permute-done.7, ...), kind=kLoop, calls=%fused_computation.124 | loop fusion | flops 17760256 | bytes 5611520 | tf_op jit(solution)/shard_map/reduce_sum | solution.py:83
  38.1 3.2 %collective-permute-start.8 = (f32[8,1,512]{2,1,0:T(1,128)S(1)}, f32[8,1,512]{2,1,0:T(1,128)S(1)}, u32[]{:S(2)}, u32[]{:S(2)}) collective-permute-start(f32[8,1,512]{2,1,0:T(1,128)S(1)} %get-tuple-element.13), channel_id=1, source_target_pairs={{32,0},{64,32},{96,64},{0,96},{33,1},{65,33},{97,65},{1,97},{34,2}... | collective-permute-start | bytes 49160 | tf_op jit(solution)/shard_map/ppermute | solution.py:26
  42.1 6.2 %collective-permute-done.10 = f32[8,128,1]{2,1,0:T(8,128)S(1)} collective-permute-done((f32[8,128,1]{2,1,0:T(8,128)S(1)}, f32[8,128,1]{2,1,0:T(8,128)S(1)}, u32[]{:S(2)}, u32[]{:S(2)}) %collective-permute-start.10) | collective-permute-done | bytes 4128 | tf_op jit(solution)/shard_map/ppermute | solution.py:26
  48.3 3.1 %collective-permute-done.11 = f32[8,128,1]{2,1,0:T(8,128)S(1)} collective-permute-done((f32[8,128,1]{2,1,0:T(8,128)S(1)}, f32[8,128,1]{2,1,0:T(8,128)S(1)}, u32[]{:S(2)}, u32[]{:S(2)}) %collective-permute-start.11) | collective-permute-done | bytes 4128 | tf_op jit(solution)/shard_map/ppermute | solution.py:25
  51.4 2.7 %fusion.25 = f32[8,128,512]{2,1,0:T(8,128)S(1)} fusion(f32[8,128,512]{2,1,0:T(8,128)S(1)} %get-tuple-element.5, f32[8,1,512]{2,1,0:T(1,128)S(1)} %collective-permute-done.8, f32[8,1,512]{2,1,0:T(1,128)S(1)} %collective-permute-done.9, f32[8,128,1]{2,1,0:T(8,128)S(1)} %collective-permute-done.11, f32[8,128,1]{2,1,0:T(8,128)S(1)} %collective-permute-done.10, ...), kind=kLoop, calls=%fused_computation.33 | loop fusion | flops 17301504 | bytes 5349376 | tf_op jit(solution)/shard_map/jit(_where)/select_n | solution.py:64
  54.2 3.2 %collective-permute-start.12 = (f32[8,1,512]{2,1,0:T(1,128)S(1)}, f32[8,1,512]{2,1,0:T(1,128)S(1)}, u32[]{:S(2)}, u32[]{:S(2)}) collective-permute-start(f32[8,1,512]{2,1,0:T(1,128)S(1)} %get-tuple-element.9), channel_id=1, source_target_pairs={{32,0},{64,32},{96,64},{0,96},{33,1},{65,33},{97,65},{1,97},{34,2}... | collective-permute-start | bytes 49160 | tf_op jit(solution)/shard_map/ppermute | solution.py:26
  57.4 1.2 %fusion.73 = (f32[8,128,1]{2,1,0:T(8,128)}, f32[8,128,1]{2,1,0:T(8,128)}) fusion(f32[8,128,512]{2,1,0:T(8,128)S(1)} %fusion.25), kind=kLoop, calls=%fused_computation.125 | loop fusion | bytes 16384 | tf_op jit(solution)/shard_map/slice | solution.py:23
  59.1 10.0 %stack.9 = f32[1,32,4,128,4]{4,3,2,1,0:T(8,128)} reshape(f32[128,512]{1,0:T(8,128)S(1)} %get-tuple-element.4) | data formatting | bytes 524288 | tf_op jit(solution)/shard_map/stack | solution.py:83
  69.1 5.2 %copy.6 = f32[1,32,4,128,4]{3,1,4,2,0:T(8,128)S(1)} copy(f32[1,32,4,128,4]{4,3,2,1,0:T(8,128)} %stack.9) | data formatting | bytes 524288 | tf_op jit(solution)/shard_map/stack | solution.py:83
  74.4 3.9 %fusion.36 = f32[128,512]{1,0:T(8,128)S(1)} fusion(f32[8,128,512]{2,1,0:T(8,128)S(1)} %fusion.25, f32[8,1,512]{2,1,0:T(1,128)S(1)} %collective-permute-done.12, f32[8,1,512]{2,1,0:T(1,128)S(1)} %collective-permute-done.13, f32[8,128,1]{2,1,0:T(8,128)} %collective-permute-done.15, f32[8,128,1]{2,1,0:T(8,128)S(1)} %collective-permute-done.14, ...), kind=kLoop, calls=%fused_computation.44 | loop fusion | flops 17760256 | bytes 3514368 | tf_op jit(solution)/shard_map/reduce_sum | solution.py:83
  78.3 10.0 %stack.10 = f32[1,32,4,128,4]{4,3,2,1,0:T(8,128)} reshape(f32[128,512]{1,0:T(8,128)S(1)} %fusion.36) | data formatting | bytes 524288 | tf_op jit(solution)/shard_map/stack | solution.py:83
  88.3 5.2 %copy.7 = f32[1,32,4,128,4]{3,1,4,2,0:T(8,128)S(1)} copy(f32[1,32,4,128,4]{4,3,2,1,0:T(8,128)} %stack.10) | data formatting | bytes 524288 | tf_op jit(solution)/shard_map/stack | solution.py:83
  93.6 10.1 %all_to_all.5 = f32[4,2,32,128]{3,2,1,0:T(8,128)S(1)} all-to-all(f32[4,2,32,128]{3,2,1,0:T(8,128)S(1)} %broadcast_in_dim.32), channel_id=1, replica_groups=mesh['gx'=4,'gy'=8,'row'=4] {'row'}, dimensions={0} | all-to-all | bytes 262144 | tf_op jit(solution)/shard_map/all_to_all | solution.py:39
  103.7 0.6 fusion.70
  (35 shorter events, 3.0 us)
Async XLA Ops:
  0.6 18.6 %copy-start = (bf16[4,8,128,512]{3,2,1,0:T(8,128)(2,1)S(1)}, bf16[4,8,128,512]{3,2,1,0:T(8,128)(2,1)}, u32[]{:S(2)}) copy-start(bf16[4,8,128,512]{3,2,1,0:T(8,128)(2,1)} %param.3) | copy-start | bytes 12582916
  2.7 16.5 %collective-permute-start.1 = (f32[8,1,512]{2,1,0:T(1,128)S(1)}, f32[8,1,512]{2,1,0:T(1,128)S(1)}, u32[]{:S(2)}, u32[]{:S(2)}) collective-permute-start(f32[8,1,512]{2,1,0:T(1,128)S(1)} %get-tuple-element.20), channel_id=1, source_target_pairs={{0,32},{32,64},{64,96},{96,0},{1,33},{33,65},{65,97},{97,1},{2,34}... | collective-permute-start | bytes 49160 | tf_op jit(solution)/shard_map/ppermute | solution.py:25
  4.4 14.8 %collective-permute-start = (f32[8,1,512]{2,1,0:T(1,128)S(1)}, f32[8,1,512]{2,1,0:T(1,128)S(1)}, u32[]{:S(2)}, u32[]{:S(2)}) collective-permute-start(f32[8,1,512]{2,1,0:T(1,128)S(1)} %get-tuple-element.21), channel_id=1, source_target_pairs={{32,0},{64,32},{96,64},{0,96},{33,1},{65,33},{97,65},{1,97},{34,2}... | collective-permute-start | bytes 49160 | tf_op jit(solution)/shard_map/ppermute | solution.py:26
  6.2 9.9 %collective-permute-start.2 = (f32[8,128,1]{2,1,0:T(8,128)S(1)}, f32[8,128,1]{2,1,0:T(8,128)S(1)}, u32[]{:S(2)}, u32[]{:S(2)}) collective-permute-start(f32[8,128,1]{2,1,0:T(8,128)S(1)} %get-tuple-element.18), channel_id=1, source_target_pairs={{4,0},{8,4},{12,8},{16,12},{20,16},{24,20},{28,24},{0,28},{5,1},{9... | collective-permute-start | bytes 12296 | tf_op jit(solution)/shard_map/ppermute | solution.py:26
  9.4 9.8 %collective-permute-start.3 = (f32[8,128,1]{2,1,0:T(8,128)S(1)}, f32[8,128,1]{2,1,0:T(8,128)S(1)}, u32[]{:S(2)}, u32[]{:S(2)}) collective-permute-start(f32[8,128,1]{2,1,0:T(8,128)S(1)} %get-tuple-element.19), channel_id=1, source_target_pairs={{0,4},{4,8},{8,12},{12,16},{16,20},{20,24},{24,28},{28,0},{1,5},{5... | collective-permute-start | bytes 12296 | tf_op jit(solution)/shard_map/ppermute | solution.py:25
  22.1 13.1 %collective-permute-start.5 = (f32[8,1,512]{2,1,0:T(1,128)S(1)}, f32[8,1,512]{2,1,0:T(1,128)S(1)}, u32[]{:S(2)}, u32[]{:S(2)}) collective-permute-start(f32[8,1,512]{2,1,0:T(1,128)S(1)} %get-tuple-element.16), channel_id=1, source_target_pairs={{0,32},{32,64},{64,96},{96,0},{1,33},{33,65},{65,97},{97,1},{2,34}... | collective-permute-start | bytes 49160 | tf_op jit(solution)/shard_map/ppermute | solution.py:25
  22.4 12.8 %collective-permute-start.4 = (f32[8,1,512]{2,1,0:T(1,128)S(1)}, f32[8,1,512]{2,1,0:T(1,128)S(1)}, u32[]{:S(2)}, u32[]{:S(2)}) collective-permute-start(f32[8,1,512]{2,1,0:T(1,128)S(1)} %get-tuple-element.17), channel_id=1, source_target_pairs={{32,0},{64,32},{96,64},{0,96},{33,1},{65,33},{97,65},{1,97},{34,2}... | collective-permute-start | bytes 49160 | tf_op jit(solution)/shard_map/ppermute | solution.py:26
  25.4 6.7 %collective-permute-start.6 = (f32[8,128,1]{2,1,0:T(8,128)S(1)}, f32[8,128,1]{2,1,0:T(8,128)S(1)}, u32[]{:S(2)}, u32[]{:S(2)}) collective-permute-start(f32[8,128,1]{2,1,0:T(8,128)S(1)} %get-tuple-element.14), channel_id=1, source_target_pairs={{4,0},{8,4},{12,8},{16,12},{20,16},{24,20},{28,24},{0,28},{5,1},{9... | collective-permute-start | bytes 12296 | tf_op jit(solution)/shard_map/ppermute | solution.py:26
  25.4 9.8 %collective-permute-start.7 = (f32[8,128,1]{2,1,0:T(8,128)S(1)}, f32[8,128,1]{2,1,0:T(8,128)S(1)}, u32[]{:S(2)}, u32[]{:S(2)}) collective-permute-start(f32[8,128,1]{2,1,0:T(8,128)S(1)} %get-tuple-element.15), channel_id=1, source_target_pairs={{0,4},{4,8},{8,12},{12,16},{16,20},{20,24},{24,28},{28,0},{1,5},{5... | collective-permute-start | bytes 12296 | tf_op jit(solution)/shard_map/ppermute | solution.py:25
  38.0 13.4 %collective-permute-start.9 = (f32[8,1,512]{2,1,0:T(1,128)S(1)}, f32[8,1,512]{2,1,0:T(1,128)S(1)}, u32[]{:S(2)}, u32[]{:S(2)}) collective-permute-start(f32[8,1,512]{2,1,0:T(1,128)S(1)} %get-tuple-element.12), channel_id=1, source_target_pairs={{0,32},{32,64},{64,96},{96,0},{1,33},{33,65},{65,97},{97,1},{2,34}... | collective-permute-start | bytes 49160 | tf_op jit(solution)/shard_map/ppermute | solution.py:25
  38.1 13.3 %collective-permute-start.8 = (f32[8,1,512]{2,1,0:T(1,128)S(1)}, f32[8,1,512]{2,1,0:T(1,128)S(1)}, u32[]{:S(2)}, u32[]{:S(2)}) collective-permute-start(f32[8,1,512]{2,1,0:T(1,128)S(1)} %get-tuple-element.13), channel_id=1, source_target_pairs={{32,0},{64,32},{96,64},{0,96},{33,1},{65,33},{97,65},{1,97},{34,2}... | collective-permute-start | bytes 49160 | tf_op jit(solution)/shard_map/ppermute | solution.py:26
  41.5 6.7 %collective-permute-start.10 = (f32[8,128,1]{2,1,0:T(8,128)S(1)}, f32[8,128,1]{2,1,0:T(8,128)S(1)}, u32[]{:S(2)}, u32[]{:S(2)}) collective-permute-start(f32[8,128,1]{2,1,0:T(8,128)S(1)} %get-tuple-element.10), channel_id=1, source_target_pairs={{4,0},{8,4},{12,8},{16,12},{20,16},{24,20},{28,24},{0,28},{5,1},{9... | collective-permute-start | bytes 12296 | tf_op jit(solution)/shard_map/ppermute | solution.py:26
  41.6 9.8 %collective-permute-start.11 = (f32[8,128,1]{2,1,0:T(8,128)S(1)}, f32[8,128,1]{2,1,0:T(8,128)S(1)}, u32[]{:S(2)}, u32[]{:S(2)}) collective-permute-start(f32[8,128,1]{2,1,0:T(8,128)S(1)} %get-tuple-element.11), channel_id=1, source_target_pairs={{0,4},{4,8},{8,12},{12,16},{16,20},{20,24},{24,28},{28,0},{1,5},{5... | collective-permute-start | bytes 12296 | tf_op jit(solution)/shard_map/ppermute | solution.py:25
  54.1 20.3 %collective-permute-start.13 = (f32[8,1,512]{2,1,0:T(1,128)S(1)}, f32[8,1,512]{2,1,0:T(1,128)S(1)}, u32[]{:S(2)}, u32[]{:S(2)}) collective-permute-start(f32[8,1,512]{2,1,0:T(1,128)S(1)} %get-tuple-element.8), channel_id=1, source_target_pairs={{0,32},{32,64},{64,96},{96,0},{1,33},{33,65},{65,97},{97,1},{2,34}... | collective-permute-start | bytes 49160 | tf_op jit(solution)/shard_map/ppermute | solution.py:25
  54.2 20.2 %collective-permute-start.12 = (f32[8,1,512]{2,1,0:T(1,128)S(1)}, f32[8,1,512]{2,1,0:T(1,128)S(1)}, u32[]{:S(2)}, u32[]{:S(2)}) collective-permute-start(f32[8,1,512]{2,1,0:T(1,128)S(1)} %get-tuple-element.9), channel_id=1, source_target_pairs={{32,0},{64,32},{96,64},{0,96},{33,1},{65,33},{97,65},{1,97},{34,2}... | collective-permute-start | bytes 49160 | tf_op jit(solution)/shard_map/ppermute | solution.py:26
  58.6 15.8 %collective-permute-start.14 = (f32[8,128,1]{2,1,0:T(8,128)}, f32[8,128,1]{2,1,0:T(8,128)S(1)}, u32[]{:S(2)}, u32[]{:S(2)}) collective-permute-start(f32[8,128,1]{2,1,0:T(8,128)} %get-tuple-element.6), channel_id=1, source_target_pairs={{4,0},{8,4},{12,8},{16,12},{20,16},{24,20},{28,24},{0,28},{5,1},{9... | collective-permute-start | bytes 12296 | tf_op jit(solution)/shard_map/ppermute | solution.py:26
  58.6 15.8 %collective-permute-start.15 = (f32[8,128,1]{2,1,0:T(8,128)}, f32[8,128,1]{2,1,0:T(8,128)}, u32[]{:S(2)}, u32[]{:S(2)}) collective-permute-start(f32[8,128,1]{2,1,0:T(8,128)} %get-tuple-element.7), channel_id=1, source_target_pairs={{0,4},{4,8},{8,12},{12,16},{16,20},{20,24},{24,28},{28,0},{1,5},{5... | collective-permute-start | bytes 12296 | tf_op jit(solution)/shard_map/ppermute | solution.py:25
where the time goes:
time: 105 us; the launch traced here: 104 us
  local copies, waits for them, and re-layouts  32.5 us (31%)
  waiting for transfers between devices  28.3 us (27%)
  starting transfers between devices  17.9 us (17%)
  other arithmetic  14.8 us (14%)
  blocking collectives  10.1 us (10%)
    another operation x4, local copies, waits for them, and re-layouts, per_device(): snapshots = jnp.stack([jnp.sum(earlier, axis=0), jnp.sum(occupied, axis=0)])  30.5 us
    ppermute x8, waiting for transfers between devices, extended(): lax.ppermute(first, axis, [(b, a) for a, b in up])  18.9 us
    ppermute x8, starting transfers between devices, extended(): lax.ppermute(first, axis, [(b, a) for a, b in up])  14.2 us
    all_to_all x1, blocking collectives, sent_to_all(): return lax.all_to_all(copies, axis, split_axis=0, concat_axis=0, tiled=True)  10.1 us
    ppermute x8, waiting for transfers between devices, extended(): lax.ppermute(last, axis, up)  9.38 us
    reduce_sum x2, other arithmetic, per_device(): snapshots = jnp.stack([jnp.sum(earlier, axis=0), jnp.sum(occupied, axis=0)])  6.6 us
    select_n x2, other arithmetic, sublattice_update(): return jnp.where(chosen[None], updated, centre)  5.34 us
    ppermute x8, starting transfers between devices, extended(): lax.ppermute(last, axis, up)  3.69 us
  transfers between devices with their start and end apart: 16, of which 6 were waited for; matrix products, arithmetic and copies ran while one was open for 16% of the time, Pallas kernels for 0%

commit v1 on v0

v1 whole, which is shorter than its diff:
```python
import functools

import jax
import jax.numpy as jnp
import numpy as np
from jax import lax
from jax.experimental import pallas as pl
from jax.experimental.pallas import tpu as pltpu
from jax.sharding import PartitionSpec as P

MESH = pl.DeviceIdType.MESH
BLOCK = 4
LEAP = 8
SCALE = float(-0.5 * np.log2(np.e))
F32 = jnp.float32
BF16 = jnp.bfloat16


def iota(shape, dim):
    return lax.broadcasted_iota(jnp.int32, shape, dim)


def new_value(x, total, u):
    gone = 0.6 - 0.6 * jnp.exp2(total)
    kept = x * gone
    return (0.1 * x + kept) + u * (0.6 * SCALE - kept) + 0.075 * total


def split_dot(x, onehot):
    high = x.astype(BF16)
    low = (x - high.astype(F32)).astype(BF16)
    return jnp.dot(high, onehot, preferred_element_type=F32) + jnp.dot(
        low, onehot, preferred_element_type=F32
    )


def split_dot_left(onehot, x):
    high = x.astype(BF16)
    low = (x - high.astype(F32)).astype(BF16)
    return jnp.dot(onehot, high, preferred_element_type=F32) + jnp.dot(
        onehot, low, preferred_element_type=F32
    )


def kernel(
    sizes,
    occ_hbm,
    u_hbm,
    cov_ref,
    proj_ref,
    occ,
    draws,
    st,
    uu,
    sums,
    rs,
    ub,
    rsums,
    cs,
    ucs,
    merged,
    side,
    vert_send,
    vert,
    diag,
    red_send,
    red,
    load_sem,
    send_sem,
    recv_sem,
    red_send_sem,
    red_recv_sem,
):
    ngx, ngy, nrow = sizes
    gx, gy, row = lax.axis_index("gx"), lax.axis_index("gy"), lax.axis_index("row")
    up, down = lax.rem(gx + ngx - 1, ngx), lax.rem(gx + 1, ngx)
    left, right = lax.rem(gy + ngy - 1, ngy), lax.rem(gy + 1, ngy)

    def load(pair):
        return (
            pltpu.make_async_copy(
                occ_hbm.at[pl.ds(2 * pair, 2)], occ.at[pl.ds(2 * pair, 2)], load_sem.at[0, pair]
            ),
            pltpu.make_async_copy(
                u_hbm.at[:, pl.ds(2 * pair, 2)],
                draws.at[:, pl.ds(2 * pair, 2)],
                load_sem.at[1, pair],
            ),
        )

    for pair in range(4):
        for copy in load(pair):
            copy.start()

    barrier = pltpu.get_barrier_semaphore()
    lattice = [
        (gx, left),
        (gx, right),
        (up, gy),
        (down, gy),
        (up, left),
        (up, right),
        (down, left),
        (down, right),
    ]
    for a, b in lattice:
        pl.semaphore_signal(barrier, inc=1, device_id=(a, b, row), device_id_type=MESH)
    peers = [lax.rem(row + d, nrow) for d in range(1, nrow)]
    for peer in peers:
        pl.semaphore_signal(barrier, inc=1, device_id=(gx, gy, peer), device_id_type=MESH)

    zeros8 = jnp.zeros((8, 128), F32)
    for which in range(2):
        for pair in range(4):
            for t in range(4):
                st[which, pair, t, 0:8, :] = zeros8
                st[which, pair, t, 136:144, :] = zeros8
                rs[which, pair, t, 0:8, :] = zeros8
                rs[which, pair, t, 32:40, :] = zeros8
        cs[which, 0:8, :] = zeros8
        cs[which, 152:160, :] = zeros8

    wide_even = ((iota((16, 512), 0) + iota((16, 512), 1)) % 2) == 0
    for pair in range(4):
        for copy in load(pair):
            copy.wait()

        def pack(c, carry, pair=pair):
            at = pl.multiple_of(c * 16, 16)
            first = occ[2 * pair, pl.ds(at, 16), :].astype(F32) * SCALE
            second = pltpu.roll(occ[2 * pair + 1, pl.ds(at, 16), :].astype(F32) * SCALE, 511, 1)
            both = (
                jnp.where(wide_even, first, second),
                jnp.where(wide_even, second, first),
            )
            for which in range(2):
                for t in range(4):
                    st[which, pair, t, pl.ds(8 + at, 16), :] = both[which][:, 128 * t : 128 * t + 128]
            for s in range(4):
                first = draws[s, 2 * pair, pl.ds(at, 16), :].astype(F32)
                second = pltpu.roll(draws[s, 2 * pair + 1, pl.ds(at, 16), :].astype(F32), 511, 1)
                chosen = (
                    jnp.where(wide_even, first, second)
                    if s % 2 == 0
                    else jnp.where(wide_even, second, first)
                )
                for t in range(4):
                    uu[s, pair, t, pl.ds(at, 16), :] = chosen[:, 128 * t : 128 * t + 128]
            return carry

        lax.fori_loop(0, 8, pack, 0)

    def source(q, pair, t, at, size):
        if q < 2:
            return st[q, pair, t, pl.ds(8 + at, size), :] * (1.0 / SCALE)
        return uu[q - 2, pair, t, pl.ds(at, size), :]

    def lanes(rows):
        lane = iota((rows, 128), 1)
        even = ((iota((rows, 128), 0) + lane) % 2) == 0
        return lane, lane % 32, even

    def merge(c, carry):
        at = pl.multiple_of(c * 16, 16)
        lane, small, even = lanes(16)
        for q in range(6):
            real0 = even if q % 2 == 0 else jnp.logical_not(even)
            early = jnp.logical_or(small < 15, jnp.logical_and(small == 15, real0))
            total = None
            for pair in range(4):
                edge = jnp.where(lane >= 64, source(q, pair, 3, at, 16), source(q, pair, 0, at, 16))
                one = jnp.where(
                    early,
                    pltpu.roll(edge, 12 + 32 * pair, 1),
                    pltpu.roll(edge, (20 + 32 * pair) % 128, 1),
                )
                total = one if total is None else jnp.where(lane // 32 == pair, one, total)
            merged[q, pl.ds(at, 16), :] = total.astype(BF16)
        return carry

    lax.fori_loop(0, 8, merge, 0)

    sub = iota((8, 128), 0)
    for end in range(2):
        at = 0 if end == 0 else 120
        mine = sub < 4 if end == 0 else sub >= 4
        for pair in range(4):
            for t in range(4):
                base = (pair * 4 + t) * 3
                for k, (one, two) in enumerate(((0, 1), (2, 3), (4, None))):
                    tile = source(one, pair, t, at, 8)
                    if two is not None:
                        tile = jnp.where(mine, tile, pltpu.roll(source(two, pair, t, at, 8), 4, 0))
                    vert_send[end, base + k] = tile.astype(BF16)
        for q in range(5):
            tile = merged[q, pl.ds(0 if end == 0 else 112, 16), :].astype(F32)
            tile = tile[0:8] if end == 0 else tile[8:16]
            vert_send[end, 48 + q] = tile.astype(BF16)

    for which in range(2):
        for pair in range(4):
            for t in range(4):
                rs[which, pair, t, 8:16, :] = st[which, pair, t, 128:136, :]
                rs[which, pair, t, 24:32, :] = st[which, pair, t, 8:16, :]

    pl.semaphore_wait(barrier, 8 + nrow - 1)

    def send(slot, src, dst, a, b):
        copy = pltpu.make_async_remote_copy(
            src_ref=src,
            dst_ref=dst,
            send_sem=send_sem.at[slot],
            recv_sem=recv_sem.at[slot],
            device_id=(a, b, row),
            device_id_type=MESH,
        )
        copy.start()
        return copy

    copies = [
        send(2, vert_send.at[1], vert.at[0], down, gy),
        send(3, vert_send.at[0], vert.at[1], up, gy),
        send(0, merged.at[pl.ds(0, 5)], side.at[0], gx, right),
        send(1, merged.at[pl.ds(0, 5)], side.at[1], gx, left),
        send(4, vert_send.at[1, pl.ds(48, 5)], diag.at[0], down, right),
        send(5, vert_send.at[1, pl.ds(48, 5)], diag.at[1], down, left),
        send(6, vert_send.at[0, pl.ds(48, 5)], diag.at[2], up, right),
        send(7, vert_send.at[0, pl.ds(48, 5)], diag.at[3], up, left),
    ]

    lane = iota((8, 128), 1)
    first_lane, last_lane = lane == 0, lane == 127

    def update_rows(array, s, at, u_of):
        x, y = s % 2, 1 - s % 2
        totals = [None] * 4
        for pair in range(4):
            centre = [array[y, pair, t, pl.ds(at, 8), :] for t in range(4)]
            on = [pltpu.roll(v, 1, 1) for v in centre]
            back = [pltpu.roll(v, 127, 1) for v in centre]
            for t in range(4):
                total = (
                    array[y, pair, t, pl.ds(at - 1, 8), :]
                    + array[y, pair, t, pl.ds(at + 1, 8), :]
                    + jnp.where(first_lane, on[(t + 3) % 4], on[t])
                    + jnp.where(last_lane, back[(t + 1) % 4], back[t])
                )
                value = new_value(array[x, pair, t, pl.ds(at, 8), :], total, u_of(pair, t))
                array[x, pair, t, pl.ds(at, 8), :] = value
                totals[t] = value if totals[t] is None else totals[t] + value
        return totals

    for s in range(4):

        def interior(c, carry, s=s):
            at = pl.multiple_of(c * 8, 8)
            totals = update_rows(st, s, 8 + at, lambda pair, t: uu[s, pair, t, pl.ds(at, 8), :])
            for t in range(4):
                sums[s, pl.ds(at, 8), 128 * t : 128 * t + 128] = totals[t]
            return carry

        lax.fori_loop(0, 16, interior, 0)

    for copy in copies:
        copy.wait()

    low = sub < 4
    for pair in range(4):
        for t in range(4):
            base = (pair * 4 + t) * 3
            for k in range(3):
                above = vert[0, base + k].astype(F32)
                below = vert[1, base + k].astype(F32)
                one = jnp.where(low, below, above)
                two = pltpu.roll(jnp.where(low, above, below), 4, 0)
                if k == 0:
                    rs[0, pair, t, 16:24, :] = one * SCALE
                    rs[1, pair, t, 16:24, :] = two * SCALE
                elif k == 1:
                    ub[0, pair, t] = one
                    ub[1, pair, t] = two
                else:
                    ub[2, pair, t] = one
    for s in range(4):
        for part in range(3):
            if s == 3 and part == 1:
                continue
            u_of = (
                lambda pair, t: uu[s, pair, t, 120:128, :],
                lambda pair, t: ub[s, pair, t],
                lambda pair, t: uu[s, pair, t, 0:8, :],
            )[part]
            totals = update_rows(rs, s, 8 + 8 * part, u_of)
            if part != 1:
                for t in range(4):
                    rsums[s, part // 2, :, 128 * t : 128 * t + 128] = totals[t]

    def strip(q, rows, own, from_left, from_right):
        _, small, even = lanes(rows)
        real0 = even if q % 2 == 0 else jnp.logical_not(even)
        take_left = jnp.logical_and(
            jnp.logical_or(small > 15, jnp.logical_and(small == 15, jnp.logical_not(real0))),
            jnp.logical_or(small < 19, jnp.logical_and(small == 19, real0)),
        )
        take_right = jnp.logical_and(
            jnp.logical_or(small > 11, jnp.logical_and(small == 11, jnp.logical_not(real0))),
            jnp.logical_or(small < 15, jnp.logical_and(small == 15, real0)),
        )
        return jnp.where(take_left, from_left, jnp.where(take_right, from_right, own))

    def put(q, at, rows, value):
        if q < 2:
            cs[q, pl.ds(8 + at, rows), :] = value * SCALE
        else:
            ucs[q - 2, pl.ds(at, rows), :] = value

    def strip_rows(c, carry):
        at = pl.multiple_of(c * 16, 16)
        for q in range(6):
            own = merged[q, pl.ds(at, 16), :].astype(F32)
            if q < 5:
                own = strip(
                    q,
                    16,
                    own,
                    side[0, q, pl.ds(at, 16), :].astype(F32),
                    side[1, q, pl.ds(at, 16), :].astype(F32),
                )
            put(q, 8 + at, 16, own)
        return carry

    lax.fori_loop(0, 8, strip_rows, 0)
    for end in range(2):
        for q in range(5):
            put(
                q,
                0 if end == 0 else 136,
                8,
                strip(
                    q,
                    8,
                    vert[end, 48 + q].astype(F32),
                    diag[2 * end, q].astype(F32),
                    diag[2 * end + 1, q].astype(F32),
                ),
            )
        ucs[3, (0 if end == 0 else 136) : (8 if end == 0 else 144), :] = zeros8

    column = iota((512, 128), 0)
    coarse = iota((512, 128), 1)
    inner = jnp.logical_and(coarse > 0, coarse < 127)
    pick0 = jnp.where(jnp.logical_and(inner, column // BLOCK == coarse), 1.0, 0.0).astype(BF16)
    pick1 = jnp.where(jnp.logical_and(inner, (column + 1) // BLOCK == coarse), 1.0, 0.0).astype(BF16)
    small = iota((128, 128), 0) % 32
    cell = iota((128, 128), 1)

    def strip_pick(shift):
        a = jnp.logical_and(cell == 127, jnp.logical_and(small >= 8 - shift, small < 12 - shift))
        b = jnp.logical_and(cell == 0, jnp.logical_and(small >= 20 - shift, small < 24 - shift))
        return jnp.where(jnp.logical_or(a, b), 1.0, 0.0).astype(BF16)

    edge0, edge1 = strip_pick(0), strip_pick(1)
    rows4 = jnp.where(iota((32, 128), 1) // BLOCK == iota((32, 128), 0), 1.0, 0.0).astype(BF16)
    tile_even = ((iota((128, 512), 0) + iota((128, 512), 1)) % 2) == 0
    strip_even = tile_even[:, 0:128]
    low_wide = iota((8, 512), 0) < 4

    def restricted(p, q):
        def whole(s):
            top = jnp.where(low_wide, rsums[s, 1], sums[s, 0:8, :])
            bottom = jnp.where(low_wide, sums[s, 120:128, :], rsums[s, 0])
            return jnp.concatenate([top, sums[s, 8:120, :], bottom], axis=0)

        even, odd = whole(p), whole(q)
        real0 = jnp.where(tile_even, even, odd)
        real1 = jnp.where(tile_even, odd, even)
        even, odd = cs[0, 16:144, :], cs[1, 16:144, :]
        strip0 = jnp.where(strip_even, even, odd)
        strip1 = jnp.where(strip_even, odd, even)
        by_column = (
            split_dot(real0, pick0)
            + split_dot(real1, pick1)
            + split_dot(strip0, edge0)
            + split_dot(strip1, edge1)
        )
        return split_dot_left(rows4, by_column)

    def share(which):
        out = []
        for d in range(1, nrow):
            copy = pltpu.make_async_remote_copy(
                src_ref=red_send.at[which],
                dst_ref=red.at[d - 1, which],
                send_sem=red_send_sem.at[which, d - 1],
                recv_sem=red_recv_sem.at[which, d - 1],
                device_id=(gx, gy, peers[d - 1]),
                device_id_type=MESH,
            )
            copy.start()
            out.append(copy)
        return out

    shared = []
    for s in range(4):
        x, y = s % 2, 1 - s % 2

        def strip_sweep(c, carry, s=s, x=x, y=y):
            at = pl.multiple_of(c * 8, 8)
            centre = cs[y, pl.ds(8 + at, 8), :]
            total = (
                cs[y, pl.ds(7 + at, 8), :]
                + cs[y, pl.ds(9 + at, 8), :]
                + pltpu.roll(centre, 1, 1)
                + pltpu.roll(centre, 127, 1)
            )
            cs[x, pl.ds(8 + at, 8), :] = new_value(
                cs[x, pl.ds(8 + at, 8), :], total, ucs[s, pl.ds(at, 8), :]
            )
            return carry

        lax.fori_loop(0, 18, strip_sweep, 0, unroll=3)
        if s % 2 == 1:
            red_send[s // 2] = restricted(s - 1, s)
            shared += share(s // 2)

    for copy in shared:
        copy.wait()
    averages = []
    for which in range(2):
        total = red_send[which]
        for d in range(1, nrow):
            total = total + red[d - 1, which]
        averages.append(total * (1.0 / (SCALE * 8 * nrow * BLOCK * BLOCK)))
    cov_ref[...] = averages[1]
    proj_ref[...] = averages[1] + (LEAP / 2.0) * (averages[1] - averages[0])


def solution(mesh):
    sizes = tuple(mesh.shape[a] for a in ("gx", "gy", "row"))
    nrow = sizes[2]

    def per_device(occupancy, random_draws):
        any_space = pl.BlockSpec(memory_space=pl.ANY)
        vmem = pl.BlockSpec(memory_space=pltpu.VMEM)
        return pl.pallas_call(
            functools.partial(kernel, sizes),
            name="burst",
            out_shape=[jax.ShapeDtypeStruct((32, 128), F32)] * 2,
            in_specs=[any_space, any_space],
            out_specs=[vmem, vmem],
            scratch_shapes=[
                pltpu.VMEM((8, 128, 512), jnp.int32),
                pltpu.VMEM((4, 8, 128, 512), BF16),
                pltpu.VMEM((2, 4, 4, 144, 128), F32),
                pltpu.VMEM((4, 4, 4, 128, 128), F32),
                pltpu.VMEM((4, 128, 512), F32),
                pltpu.VMEM((2, 4, 4, 40, 128), F32),
                pltpu.VMEM((3, 4, 4, 8, 128), F32),
                pltpu.VMEM((4, 2, 8, 512), F32),
                pltpu.VMEM((2, 160, 128), F32),
                pltpu.VMEM((4, 144, 128), F32),
                pltpu.VMEM((6, 128, 128), BF16),
                pltpu.VMEM((2, 5, 128, 128), BF16),
                pltpu.VMEM((2, 53, 8, 128), BF16),
                pltpu.VMEM((2, 53, 8, 128), BF16),
                pltpu.VMEM((4, 5, 8, 128), BF16),
                pltpu.VMEM((2, 32, 128), F32),
                pltpu.VMEM((nrow - 1, 2, 32, 128), F32),
                pltpu.SemaphoreType.DMA((2, 4)),
                pltpu.SemaphoreType.DMA((8,)),
                pltpu.SemaphoreType.DMA((8,)),
                pltpu.SemaphoreType.DMA((2, nrow - 1)),
                pltpu.SemaphoreType.DMA((2, nrow - 1)),
            ],
            compiler_params=pltpu.CompilerParams(
                collective_id=0, has_side_effects=True, vmem_limit_bytes=48 * 1024 * 1024
            ),
        )(occupancy, random_draws)

    return jax.shard_map(
        per_device,
        mesh=mesh,
        in_specs=(P("row", "gx", "gy"), P(None, "row", "gx", "gy")),
        out_specs=(P("gx", "gy"), P("gx", "gy")),
        check_vma=False,
    )
```

time: 105 us -> 27.2 us (0.26)
  local copies, waits for them, and re-layouts: 32.5 us -> 2.8 us
  waiting for transfers between devices: 28.3 us -> 0 us
  Pallas kernels: 0 us -> 23.6 us
  starting transfers between devices: 17.9 us -> 0 us
  other arithmetic: 14.8 us -> 0 us
  blocking collectives: 10.1 us -> 0 us
    another operation x4 -> x0, local copies, waits for them, and re-layouts: 30.5 us -> none  [per_device(): snapshots = jnp.stack([jnp.sum(earlier, axis=0), jnp.sum(occupied, axis=0)])]
    ppermute x16 -> x0, waiting for transfers between devices: 28.3 us -> none  [the longest x8 18.9 us: extended(): lax.ppermute(first, axis, [(b, a) for a, b in up])]
    pallas_call x0 -> x1, Pallas kernels: none -> 23.6 us  [per_device(): pl.pallas_call(functools.partial(kernel, sizes), name='burst', out_shape=...]
    ppermute x16 -> x0, starting transfers between devices: 17.9 us -> none  [the longest x8 14.2 us: extended(): lax.ppermute(first, axis, [(b, a) for a, b in up])]
    all_to_all x1 -> x0, blocking collectives: 10.1 us -> none  [sent_to_all(): return lax.all_to_all(copies, axis, split_axis=0, concat_axis=0, tiled=True)]
    reduce_sum x4 -> x0, other arithmetic: 6.65 us -> none  [the longest x2 6.6 us: per_device(): snapshots = jnp.stack([jnp.sum(earlier, axis=0), jnp.sum(occupied, axis=0)])]
    select_n x2 -> x0, other arithmetic: 5.34 us -> none  [sublattice_update(): return jnp.where(chosen[None], updated, centre)]
    unnamed x2 -> x4, local copies, waits for them, and re-layouts: 0.01 us -> 2.8 us
  transfers between devices with their start and end apart: 16 -> 0, of which waited for: 6 -> 0; matrix products, arithmetic and copies ran while one was open for 16% -> 0% of each run, Pallas kernels for 0% -> 0%
where the time goes in v1:
time: 27.2 us; the launch traced here: 27.1 us
  Pallas kernels  23.6 us (87%)
  local copies, waits for them, and re-layouts  2.8 us (10%)
  between operations  0.65 us (2%)
    pallas_call x1, Pallas kernels, per_device(): pl.pallas_call(functools.partial(kernel, sizes), name='burst', out_shape=...  23.6 us
    unnamed x4, local copies, waits for them, and re-layouts  2.8 us

profile of v1, /device:TPU:0, one launch (start us, length us, event | category | flops | bytes accessed | tf_op | source)
XLA Modules:
  0.0 27.1 jit_solution(8783441387097161582)
XLA Ops:
  0.6 0.0 copy-start
  0.6 1.6 %copy-done = s32[8,128,512]{2,1,0:T(8,128)S(1)} copy-done((s32[8,128,512]{2,1,0:T(8,128)S(1)}, s32[8,128,512]{2,1,0:T(8,128)}, u32[]{:S(2)}) %copy-start) | copy-done | bytes 2097176
  2.2 23.6 %burst.1 = (f32[32,128]{1,0:T(8,128)S(1)}, f32[32,128]{1,0:T(8,128)S(1)}) custom-call(s32[8,128,512]{2,1,0:T(8,128)S(1)} %copy-done, bf16[4,8,128,512]{3,2,1,0:T(8,128)(2,1)} %u_hbm.1), custom_call_target="tpu_custom_call" | custom-call | tf_op jit(solution)/shard_map/burst/pallas_call | solution.py:445
  25.8 0.6 %copy.6 = f32[32,128]{1,0:T(8,128)} copy(f32[32,128]{1,0:T(8,128)S(1)} %get-tuple-element.4) | data formatting | bytes 32768
  26.5 0.6 %copy.7 = f32[32,128]{1,0:T(8,128)} copy(f32[32,128]{1,0:T(8,128)S(1)} %get-tuple-element.5) | data formatting | bytes 32768
Async XLA Ops:
  0.6 1.6 %copy-start = (s32[8,128,512]{2,1,0:T(8,128)S(1)}, s32[8,128,512]{2,1,0:T(8,128)}, u32[]{:S(2)}) copy-start(s32[8,128,512]{2,1,0:T(8,128)} %occ_hbm.1) | copy-start | bytes 6291460

commit v2 on v1

--- a/solution.py
+++ b/solution.py
@@ -46,8 +46,7 @@
     sizes,
     occ_hbm,
     u_hbm,
-    cov_ref,
-    proj_ref,
+    average_ref,
     occ,
     draws,
     st,
@@ -148,7 +147,7 @@
                     uu[s, pair, t, pl.ds(at, 16), :] = chosen[:, 128 * t : 128 * t + 128]
             return carry
 
-        lax.fori_loop(0, 8, pack, 0)
+        lax.fori_loop(0, 8, pack, 0, unroll=4)
 
     def source(q, pair, t, at, size):
         if q < 2:
@@ -178,7 +177,7 @@
             merged[q, pl.ds(at, 16), :] = total.astype(BF16)
         return carry
 
-    lax.fori_loop(0, 8, merge, 0)
+    lax.fori_loop(0, 8, merge, 0, unroll=2)
 
     sub = iota((8, 128), 0)
     for end in range(2):
@@ -259,7 +258,7 @@
                 sums[s, pl.ds(at, 8), 128 * t : 128 * t + 128] = totals[t]
             return carry
 
-        lax.fori_loop(0, 16, interior, 0)
+        lax.fori_loop(0, 16, interior, 0, unroll=16)
 
     for copy in copies:
         copy.wait()
@@ -329,7 +328,7 @@
             put(q, 8 + at, 16, own)
         return carry
 
-    lax.fori_loop(0, 8, strip_rows, 0)
+    lax.fori_loop(0, 8, strip_rows, 0, unroll=2)
     for end in range(2):
         for q in range(5):
             put(
@@ -418,21 +417,18 @@
             )
             return carry
 
-        lax.fori_loop(0, 18, strip_sweep, 0, unroll=3)
+        lax.fori_loop(0, 18, strip_sweep, 0, unroll=18)
         if s % 2 == 1:
             red_send[s // 2] = restricted(s - 1, s)
             shared += share(s // 2)
 
     for copy in shared:
         copy.wait()
-    averages = []
     for which in range(2):
         total = red_send[which]
         for d in range(1, nrow):
             total = total + red[d - 1, which]
-        averages.append(total * (1.0 / (SCALE * 8 * nrow * BLOCK * BLOCK)))
-    cov_ref[...] = averages[1]
-    proj_ref[...] = averages[1] + (LEAP / 2.0) * (averages[1] - averages[0])
+        average_ref[which] = total * (1.0 / (SCALE * 8 * nrow * BLOCK * BLOCK))
 
 
 def solution(mesh):
@@ -442,12 +438,12 @@
     def per_device(occupancy, random_draws):
         any_space = pl.BlockSpec(memory_space=pl.ANY)
         vmem = pl.BlockSpec(memory_space=pltpu.VMEM)
-        return pl.pallas_call(
+        averages = pl.pallas_call(
             functools.partial(kernel, sizes),
             name="burst",
-            out_shape=[jax.ShapeDtypeStruct((32, 128), F32)] * 2,
+            out_shape=jax.ShapeDtypeStruct((2, 32, 128), F32),
             in_specs=[any_space, any_space],
-            out_specs=[vmem, vmem],
+            out_specs=vmem,
             scratch_shapes=[
                 pltpu.VMEM((8, 128, 512), jnp.int32),
                 pltpu.VMEM((4, 8, 128, 512), BF16),
@@ -473,9 +469,11 @@
                 pltpu.SemaphoreType.DMA((2, nrow - 1)),
             ],
             compiler_params=pltpu.CompilerParams(
-                collective_id=0, has_side_effects=True, vmem_limit_bytes=48 * 1024 * 1024
+                collective_id=0, has_side_effects=True, vmem_limit_bytes=62 * 1024 * 1024
             ),
         )(occupancy, random_draws)
+        coverage = averages[1]
+        return coverage, coverage + (LEAP / 2.0) * (coverage - averages[0])
 
     return jax.shard_map(
         per_device,

time: 27.2 us -> 22.8 us (0.84)
  Pallas kernels: 23.6 us -> 20.7 us
  local copies, waits for them, and re-layouts: 2.8 us -> 0 us
  other arithmetic: 0 us -> 1.35 us
    pallas_call x1, Pallas kernels: 23.6 us -> 20.7 us  [per_device(): pl.pallas_call(functools.partial(kernel, sizes), name='burst', out_shape=...]
    unnamed x4 -> x0, local copies, waits for them, and re-layouts: 2.8 us -> none
    add x0 -> x1, other arithmetic: none -> 1.35 us  [per_device(): return (coverage, coverage + LEAP / 2.0 * (coverage - averages[0]))]
where the time goes in v2:
time: 22.8 us; the launch traced here: 22.7 us
  Pallas kernels  20.7 us (91%)
  other arithmetic  1.35 us (6%)
  between operations  0.64 us (3%)
    pallas_call x1, Pallas kernels, per_device(): pl.pallas_call(functools.partial(kernel, sizes), name='burst', out_shape=...  20.7 us
    add x1, other arithmetic, per_device(): return (coverage, coverage + LEAP / 2.0 * (coverage - averages[0]))  1.35 us

profile of v2, /device:TPU:0, one launch (start us, length us, event | category | flops | bytes accessed | tf_op | source)
XLA Modules:
  0.0 22.7 jit_solution(13473429235574152961)
XLA Ops:
  0.6 20.7 %burst.1 = f32[2,32,128]{2,1,0:T(8,128)} custom-call(s32[8,128,512]{2,1,0:T(8,128)} %occ_hbm.1, bf16[4,8,128,512]{3,2,1,0:T(8,128)(2,1)} %u_hbm.1), custom_call_target="tpu_custom_call" | custom-call | tf_op jit(solution)/shard_map/burst/pallas_call | solution.py:441
  21.3 1.4 %fusion.1 = (f32[32,128]{1,0:T(8,128)}, f32[32,128]{1,0:T(8,128)}) fusion(f32[2,32,128]{2,1,0:T(8,128)} %burst.1), kind=kLoop, calls=%fused_computation.2 | loop fusion | flops 12288 | bytes 65536 | tf_op jit(solution)/shard_map/add | solution.py:476

commit v3 on v2

v3 whole, which is shorter than its diff:
```python
import functools

import jax
import jax.numpy as jnp
import numpy as np
from jax import lax
from jax.experimental import pallas as pl
from jax.experimental.pallas import tpu as pltpu
from jax.sharding import PartitionSpec as P

MESH = pl.DeviceIdType.MESH
BLOCK = 4
LEAP = 8
SCALE = float(-0.5 * np.log2(np.e))
F32 = jnp.float32
BF16 = jnp.bfloat16


def iota(shape, dim):
    return lax.broadcasted_iota(jnp.int32, shape, dim)


def new_value(x, total, u):
    gone = 0.6 - 0.6 * jnp.exp2(total)
    kept = x * gone
    return (0.1 * x + kept) + u * (0.6 * SCALE - kept) + 0.075 * total


def split_dot(x, onehot):
    high = x.astype(BF16)
    low = (x - high.astype(F32)).astype(BF16)
    return jnp.dot(high, onehot, preferred_element_type=F32) + jnp.dot(
        low, onehot, preferred_element_type=F32
    )


def split_dot_left(onehot, x):
    high = x.astype(BF16)
    low = (x - high.astype(F32)).astype(BF16)
    return jnp.dot(onehot, high, preferred_element_type=F32) + jnp.dot(
        onehot, low, preferred_element_type=F32
    )


def kernel(
    sizes,
    occ_hbm,
    u_hbm,
    average_ref,
    occ,
    draws,
    st,
    uu,
    sums,
    rs,
    ub,
    rsums,
    cs,
    ucs,
    place,
    pick,
    edge_pick,
    merged,
    side_send,
    side,
    corner_send,
    corner,
    vert_send,
    vert,
    main_part,
    red_send,
    red,
    load_sem,
    send_sem,
    recv_sem,
    red_send_sem,
    red_recv_sem,
):
    ngx, ngy, nrow = sizes
    gx, gy, row = lax.axis_index("gx"), lax.axis_index("gy"), lax.axis_index("row")
    up, down = lax.rem(gx + ngx - 1, ngx), lax.rem(gx + 1, ngx)
    left, right = lax.rem(gy + ngy - 1, ngy), lax.rem(gy + 1, ngy)

    loads = []

    def load(group, src, dst):
        copy = pltpu.make_async_copy(src, dst, load_sem.at[len(loads)])
        copy.start()
        loads.append((group, copy))

    def arrived(group):
        for which, copy in loads:
            if which == group:
                copy.wait()

    def load_occ(group, reals, rows, columns):
        at = (pl.ds(*reals), pl.ds(*rows), pl.ds(*columns))
        load(group, occ_hbm.at[at], occ.at[at])

    def load_u(group, sweeps, reals, rows, columns):
        at = (pl.ds(*sweeps), pl.ds(*reals), pl.ds(*rows), pl.ds(*columns))
        load(group, u_hbm.at[at], draws.at[at])

    load_occ("pair0", (0, 2), (0, 128), (0, 512))
    load_u("pair0", (0, 4), (0, 2), (0, 128), (0, 512))
    for columns in ((0, 128), (384, 128)):
        load_occ("edges", (2, 6), (0, 128), columns)
        load_u("edges", (0, 4), (2, 6), (0, 128), columns)
    for rows in ((0, 16), (112, 16)):
        load_occ("edges", (2, 6), rows, (128, 256))
        load_u("edges", (0, 3), (2, 6), rows, (128, 256))
    for pair in range(1, 4):
        load_occ("pair%d" % pair, (2 * pair, 2), (16, 96), (128, 256))
        load_u("pair%d" % pair, (0, 3), (2 * pair, 2), (16, 96), (128, 256))
        load_u("pair%d" % pair, (3, 1), (2 * pair, 2), (0, 128), (128, 256))

    barrier = pltpu.get_barrier_semaphore()
    lattice = [
        (gx, left),
        (gx, right),
        (up, gy),
        (down, gy),
        (up, left),
        (up, right),
        (down, left),
        (down, right),
    ]
    for a, b in lattice:
        pl.semaphore_signal(barrier, inc=1, device_id=(a, b, row), device_id_type=MESH)
    peers = [lax.rem(row + d, nrow) for d in range(1, nrow)]
    for peer in peers:
        pl.semaphore_signal(barrier, inc=1, device_id=(gx, gy, peer), device_id_type=MESH)

    zeros8 = jnp.zeros((8, 128), F32)
    for which in range(2):
        for pair in range(4):
            for t in range(4):
                st[which, pair, t, 0:8, :] = zeros8
                st[which, pair, t, 136:144, :] = zeros8
                rs[which, pair, t, 0:8, :] = zeros8
                rs[which, pair, t, 32:40, :] = zeros8
        cs[which, 0:8, :] = zeros8
        cs[which, 152:160, :] = zeros8
    ucs[3, 0:8, :] = zeros8
    ucs[3, 136:144, :] = zeros8

    k = iota((256, 128), 0)
    far = k - 128
    for real in range(2):
        for pair in range(4):
            to = iota((256, 128), 1) - 32 * pair + real
            hit = ((k < 4) & (to == k + 12)) | ((k < 8) & (to == k + 20))
            hit |= ((far >= 120) & (to == far - 116)) | ((far >= 124) & (to == far - 108))
            place[real, 256 * pair : 256 * pair + 256, :] = jnp.where(hit, 1.0, 0.0).astype(BF16)
        column = iota((512, 128), 0) + real
        coarse = iota((512, 128), 1)
        hit = (coarse > 0) & (coarse < 127) & (column // BLOCK == coarse)
        pick[real] = jnp.where(hit, 1.0, 0.0).astype(BF16)
        small = iota((128, 128), 0) % 32 + real
        cell = iota((128, 128), 1)
        hit = ((cell == 127) & (small >= 8) & (small < 12)) | (
            (cell == 0) & (small >= 20) & (small < 24)
        )
        edge_pick[real] = jnp.where(hit, 1.0, 0.0).astype(BF16)

    sub = iota((8, 128), 0)
    low = sub < 4
    lane = iota((8, 128), 1)
    first_lane, last_lane = lane == 0, lane == 127
    wide_even = ((iota((16, 512), 0) + iota((16, 512), 1)) % 2) == 0
    tile_even = ((iota((128, 128), 0) + iota((128, 128), 1)) % 2) == 0

    def update_rows(array, s, at, pairs, u_of):
        x, y = s % 2, 1 - s % 2
        totals = [None] * 4
        for pair in pairs:
            centre = [array[y, pair, t, pl.ds(at, 8), :] for t in range(4)]
            on = [pltpu.roll(v, 1, 1) for v in centre]
            back = [pltpu.roll(v, 127, 1) for v in centre]
            for t in range(4):
                total = (
                    array[y, pair, t, pl.ds(at - 1, 8), :]
                    + array[y, pair, t, pl.ds(at + 1, 8), :]
                    + jnp.where(first_lane, on[(t + 3) % 4], on[t])
                    + jnp.where(last_lane, back[(t + 1) % 4], back[t])
                )
                value = new_value(array[x, pair, t, pl.ds(at, 8), :], total, u_of(pair, t))
                array[x, pair, t, pl.ds(at, 8), :] = value
                totals[t] = value if totals[t] is None else totals[t] + value
        return totals

    def paired(first, second, even, which):
        shifted = pltpu.roll(second, 511, 1)
        return jnp.where(even, first, shifted) if which == 0 else jnp.where(even, shifted, first)

    def pack(pair):
        def rows(c, carry):
            at = pl.multiple_of(c * 16, 16)
            first = occ[2 * pair, pl.ds(at, 16), :].astype(F32) * SCALE
            second = occ[2 * pair + 1, pl.ds(at, 16), :].astype(F32) * SCALE
            for which in range(2):
                both = paired(first, second, wide_even, which)
                for t in range(4):
                    st[which, pair, t, pl.ds(8 + at, 16), :] = both[:, 128 * t : 128 * t + 128]
            for s in range(4):
                first = draws[s, 2 * pair, pl.ds(at, 16), :].astype(F32)
                second = draws[s, 2 * pair + 1, pl.ds(at, 16), :].astype(F32)
                both = paired(first, second, wide_even, s % 2)
                for t in range(4):
                    uu[s, pair, t, pl.ds(at, 16), :] = both[:, 128 * t : 128 * t + 128]
            return carry

        lax.fori_loop(0, 8, rows, 0, unroll=4)
        for which in range(2):
            for t in range(4):
                rs[which, pair, t, 8:16, :] = st[which, pair, t, 128:136, :]
                rs[which, pair, t, 24:32, :] = st[which, pair, t, 8:16, :]

    def interior(pair):
        for s in range(4):

            def rows(c, carry, s=s):
                at = pl.multiple_of(c * 8, 8)
                totals = update_rows(
                    st, s, 8 + at, (pair,), lambda p, t: uu[s, p, t, pl.ds(at, 8), :]
                )
                for t in range(4):
                    columns = slice(128 * t, 128 * t + 128)
                    if pair == 0:
                        sums[s, pl.ds(at, 8), columns] = totals[t]
                    else:
                        sums[s, pl.ds(at, 8), columns] += totals[t]
                return carry

            lax.fori_loop(0, 16, rows, 0, unroll=16)

    arrived("pair0")
    pack(0)
    interior(0)
    arrived("edges")

    def edge_columns(real, load_real):
        tiles = []
        for pair in range(4):
            tiles += [load_real(2 * pair + real, 0), load_real(2 * pair + real, 384)]
        return jnp.dot(
            jnp.concatenate(tiles, axis=1), place[real], preferred_element_type=F32
        )

    def put_merged(q, value):
        merged[q] = value.astype(BF16)
        return value

    wholes = [edge_columns(r, lambda i, c: occ[i, :, c : c + 128].astype(F32).astype(BF16)) for r in (0, 1)]
    strips = [
        put_merged(0, jnp.where(tile_even, wholes[0], wholes[1])),
        put_merged(1, jnp.where(tile_even, wholes[1], wholes[0])),
    ]
    for s in range(4):
        wholes = [edge_columns(r, lambda i, c: draws[s, i, :, c : c + 128]) for r in (0, 1)]
        strips.append(
            put_merged(2 + s, jnp.where(tile_even, wholes[s % 2], wholes[1 - s % 2]))
        )
    slot = (iota((128, 128), 1) % 32) // 9
    sent = (
        jnp.where(
            slot == 0,
            pltpu.roll(strips[0], 117, 1),
            jnp.where(slot == 1, pltpu.roll(strips[1], 126, 1), pltpu.roll(strips[2], 7, 1)),
        ),
        jnp.where(slot == 0, pltpu.roll(strips[3], 117, 1), pltpu.roll(strips[4], 126, 1)),
    )
    for part in range(2):
        side_send[part] = sent[part].astype(BF16)
        corner_send[0, part] = sent[part][0:8].astype(BF16)
        corner_send[1, part] = sent[part][120:128].astype(BF16)
    for q in range(5):
        vert_send[0, 32 + q] = strips[q][0:8].astype(BF16)
        vert_send[1, 32 + q] = strips[q][120:128].astype(BF16)

    even8 = wide_even[0:8]
    sub_wide = iota((8, 512), 0)
    for end in range(2):
        at = 0 if end == 0 else 112
        keep = slice(0, 8) if end == 0 else slice(8, 16)
        mine = sub_wide < 4 if end == 0 else sub_wide >= 4
        outer = sub_wide == (7 if end == 0 else 0)
        for pair in range(4):
            first = occ[2 * pair, at : at + 16, :][keep].astype(F32)
            second = occ[2 * pair + 1, at : at + 16, :][keep].astype(F32)
            p, q = paired(first, second, even8, 0), paired(first, second, even8, 1)
            u = [
                paired(
                    draws[s, 2 * pair, at : at + 16, :].astype(F32)[keep],
                    draws[s, 2 * pair + 1, at : at + 16, :].astype(F32)[keep],
                    even8,
                    s % 2,
                )
                for s in range(3)
            ]
            tiles = (
                jnp.where(
                    mine,
                    q,
                    jnp.where(outer, pltpu.roll(u[2], 7 if end == 0 else 1, 0), pltpu.roll(u[0], 4, 0)),
                ),
                jnp.where(mine, p, pltpu.roll(u[1], 4, 0)),
            )
            for n in range(2):
                packed = tiles[n].astype(BF16)
                for t in range(4):
                    vert_send[end, 8 * pair + 2 * t + n] = packed[:, 128 * t : 128 * t + 128]

    pl.semaphore_wait(barrier, 8 + nrow - 1)

    def send(slot, src, dst, a, b):
        copy = pltpu.make_async_remote_copy(
            src_ref=src,
            dst_ref=dst,
            send_sem=send_sem.at[slot],
            recv_sem=recv_sem.at[slot],
            device_id=(a, b, row),
            device_id_type=MESH,
        )
        copy.start()
        return copy

    copies = [
        send(4, corner_send.at[1], corner.at[0], down, right),
        send(5, corner_send.at[1], corner.at[1], down, left),
        send(6, corner_send.at[0], corner.at[2], up, right),
        send(7, corner_send.at[0], corner.at[3], up, left),
        send(2, vert_send.at[1], vert.at[0], down, gy),
        send(3, vert_send.at[0], vert.at[1], up, gy),
        send(0, side_send, side.at[0], gx, right),
        send(1, side_send, side.at[1], gx, left),
    ]

    for pair in range(1, 4):
        arrived("pair%d" % pair)
        pack(pair)
        interior(pair)

    coarse_row = iota((32, 128), 0)
    all_rows = iota((32, 128), 1) // BLOCK == coarse_row
    rows_all = jnp.where(all_rows, 1.0, 0.0).astype(BF16)
    rows_inner = jnp.where(all_rows & (coarse_row > 0) & (coarse_row < 31), 1.0, 0.0).astype(BF16)
    even_wide = ((iota((128, 512), 0) + iota((128, 512), 1)) % 2) == 0

    for which in range(2):
        p, q = sums[2 * which], sums[2 * which + 1]
        by_column = split_dot(jnp.where(even_wide, p, q), pick[0]) + split_dot(
            jnp.where(even_wide, q, p), pick[1]
        )
        main_part[which] = split_dot_left(rows_inner, by_column)

    for copy in copies:
        copy.wait()

    for pair in range(4):
        for t in range(4):
            base = 8 * pair + 2 * t
            above, below = vert[0, base].astype(F32), vert[1, base].astype(F32)
            rs[1, pair, t, 16:24, :] = jnp.where(low, below, above) * SCALE
            other = jnp.where(low, above, below)
            ub[0, pair, t] = pltpu.roll(other, 4, 0)
            ub[2, pair, t] = jnp.where(low, pltpu.roll(other, 1, 0), pltpu.roll(other, 7, 0))
            above, below = vert[0, base + 1].astype(F32), vert[1, base + 1].astype(F32)
            rs[0, pair, t, 16:24, :] = jnp.where(low, below, above) * SCALE
            ub[1, pair, t] = pltpu.roll(jnp.where(low, above, below), 4, 0)

    def strip(q, own, from_left, from_right):
        shape = own.shape
        small = iota(shape, 1) % 32
        even = ((iota(shape, 0) + small) % 2) == 0
        real0 = even if q % 2 == 0 else jnp.logical_not(even)
        real1 = jnp.logical_not(real0)
        back = (11, 2, 121, 11, 2)[q]
        take_left = ((small > 15) | ((small == 15) & real1)) & ((small < 19) | ((small == 19) & real0))
        take_right = ((small > 11) | ((small == 11) & real1)) & ((small < 15) | ((small == 15) & real0))
        return jnp.where(
            take_left,
            pltpu.roll(from_left, back, 1),
            jnp.where(take_right, pltpu.roll(from_right, back, 1), own),
        )

    def put(q, at, value):
        rows = value.shape[0]
        if q < 2:
            cs[q, 8 + at : 8 + at + rows, :] = value * SCALE
        else:
            ucs[q - 2, at : at + rows, :] = value

    def part_of(q):
        return 0 if q < 3 else 1

    for q in range(5):
        n = part_of(q)
        put(
            q,
            8,
            strip(q, merged[q].astype(F32), side[0, n].astype(F32), side[1, n].astype(F32)),
        )
        for end in range(2):
            put(
                q,
                0 if end == 0 else 136,
                strip(
                    q,
                    vert[end, 32 + q].astype(F32),
                    corner[2 * end, n].astype(F32),
                    corner[2 * end + 1, n].astype(F32),
                ),
            )
    put(5, 8, merged[5].astype(F32))

    def share(which):
        out = []
        for d in range(1, nrow):
            copy = pltpu.make_async_remote_copy(
                src_ref=red_send.at[which],
                dst_ref=red.at[d - 1, which],
                send_sem=red_send_sem.at[which, d - 1],
                recv_sem=red_recv_sem.at[which, d - 1],
                device_id=(gx, gy, peers[d - 1]),
                device_id_type=MESH,
            )
            copy.start()
            out.append(copy)
        return out

    def edge_part(which):
        p, q = 2 * which, 2 * which + 1
        even = jnp.concatenate([rsums[p, 1], rsums[p, 0]], axis=0)
        odd = jnp.concatenate([rsums[q, 1], rsums[q, 0]], axis=0)
        by_row = split_dot(jnp.where(wide_even, even, odd), pick[0]) + split_dot(
            jnp.where(wide_even, odd, even), pick[1]
        )
        even, odd = cs[0, 16:144, :], cs[1, 16:144, :]
        by_column = split_dot(jnp.where(tile_even, even, odd), edge_pick[0]) + split_dot(
            jnp.where(tile_even, odd, even), edge_pick[1]
        )
        top = by_column[0:8] + jnp.where(low, by_row[0:8], 0.0)
        bottom = by_column[120:128] + jnp.where(low, 0.0, by_row[8:16])
        by_column = jnp.concatenate([top, by_column[8:120], bottom], axis=0)
        return split_dot_left(rows_all, by_column)

    shared = []
    for s in range(4):
        x, y = s % 2, 1 - s % 2
        for part in range(3):
            if s == 3 and part == 1:
                continue
            u_of = (
                lambda pair, t: uu[s, pair, t, 120:128, :],
                lambda pair, t: ub[s, pair, t],
                lambda pair, t: uu[s, pair, t, 0:8, :],
            )[part]
            totals = update_rows(rs, s, 8 + 8 * part, range(4), u_of)
            if part != 1:
                for t in range(4):
                    rsums[s, part // 2, :, 128 * t : 128 * t + 128] = totals[t]
        for at in range(0, 144, 8):
            centre = cs[y, 8 + at : 16 + at, :]
            total = (
                cs[y, 7 + at : 15 + at, :]
                + cs[y, 9 + at : 17 + at, :]
                + pltpu.roll(centre, 1, 1)
                + pltpu.roll(centre, 127, 1)
            )
            cs[x, 8 + at : 16 + at, :] = new_value(
                cs[x, 8 + at : 16 + at, :], total, ucs[s, at : at + 8, :]
            )
        if s % 2 == 1:
            red_send[s // 2] = main_part[s // 2] + edge_part(s // 2)
            shared += share(s // 2)

    for copy in shared:
        copy.wait()
    for which in range(2):
        total = red_send[which]
        for d in range(1, nrow):
            total = total + red[d - 1, which]
        average_ref[which] = total * (1.0 / (SCALE * 8 * nrow * BLOCK * BLOCK))


def solution(mesh):
    sizes = tuple(mesh.shape[a] for a in ("gx", "gy", "row"))
    nrow = sizes[2]

    def per_device(occupancy, random_draws):
        any_space = pl.BlockSpec(memory_space=pl.ANY)
        vmem = pl.BlockSpec(memory_space=pltpu.VMEM)
        averages = pl.pallas_call(
            functools.partial(kernel, sizes),
            name="burst",
            out_shape=pltpu.VMEM((2, 32, 128), F32),
            in_specs=[any_space, any_space],
            out_specs=vmem,
            scratch_shapes=[
                pltpu.VMEM((8, 128, 512), jnp.int32),
                pltpu.VMEM((4, 8, 128, 512), BF16),
                pltpu.VMEM((2, 4, 4, 144, 128), F32),
                pltpu.VMEM((4, 4, 4, 128, 128), F32),
                pltpu.VMEM((4, 128, 512), F32),
                pltpu.VMEM((2, 4, 4, 40, 128), F32),
                pltpu.VMEM((3, 4, 4, 8, 128), F32),
                pltpu.VMEM((4, 2, 8, 512), F32),
                pltpu.VMEM((2, 160, 128), F32),
                pltpu.VMEM((4, 144, 128), F32),
                pltpu.VMEM((2, 1024, 128), BF16),
                pltpu.VMEM((2, 512, 128), BF16),
                pltpu.VMEM((2, 128, 128), BF16),
                pltpu.VMEM((6, 128, 128), BF16),
                pltpu.VMEM((2, 128, 128), BF16),
                pltpu.VMEM((2, 2, 128, 128), BF16),
                pltpu.VMEM((2, 2, 8, 128), BF16),
                pltpu.VMEM((4, 2, 8, 128), BF16),
                pltpu.VMEM((2, 37, 8, 128), BF16),
                pltpu.VMEM((2, 37, 8, 128), BF16),
                pltpu.VMEM((2, 32, 128), F32),
                pltpu.VMEM((2, 32, 128), F32),
                pltpu.VMEM((nrow - 1, 2, 32, 128), F32),
                pltpu.SemaphoreType.DMA((19,)),
                pltpu.SemaphoreType.DMA((8,)),
                pltpu.SemaphoreType.DMA((8,)),
                pltpu.SemaphoreType.DMA((2, nrow - 1)),
                pltpu.SemaphoreType.DMA((2, nrow - 1)),
            ],
            compiler_params=pltpu.CompilerParams(
                collective_id=0, has_side_effects=True, vmem_limit_bytes=62 * 1024 * 1024
            ),
        )(occupancy, random_draws)
        coverage = averages[1]
        return coverage, coverage + (LEAP / 2.0) * (coverage - averages[0])

    return jax.shard_map(
        per_device,
        mesh=mesh,
        in_specs=(P("row", "gx", "gy"), P(None, "row", "gx", "gy")),
        out_specs=(P("gx", "gy"), P("gx", "gy")),
        check_vma=False,
    )
```

time: 22.8 us -> 19 us (0.83)
  Pallas kernels: 20.7 us -> 17.6 us
  other arithmetic: 1.35 us -> 0.62 us
    pallas_call x1, Pallas kernels: 20.7 us -> 17.6 us  [per_device(): pl.pallas_call(functools.partial(kernel, sizes), name='burst', out_shape=...]
    add x1, other arithmetic: 1.35 us -> 0.62 us  [per_device(): return (coverage, coverage + LEAP / 2.0 * (coverage - averages[0]))]
where the time goes in v3:
time: 19 us; the launch traced here: 18.9 us
  Pallas kernels  17.6 us (93%)
  between operations  0.64 us (3%)
  other arithmetic  0.62 us (3%)
    pallas_call x1, Pallas kernels, per_device(): pl.pallas_call(functools.partial(kernel, sizes), name='burst', out_shape=...  17.6 us
    add x1, other arithmetic, per_device(): return (coverage, coverage + LEAP / 2.0 * (coverage - averages[0]))  0.62 us

profile of v3, /device:TPU:0, one launch (start us, length us, event | category | flops | bytes accessed | tf_op | source)
XLA Modules:
  0.0 18.9 jit_solution(7564294415093735770)
XLA Ops:
  0.6 17.6 %burst.1 = f32[2,32,128]{2,1,0:T(8,128)S(1)} custom-call(s32[8,128,512]{2,1,0:T(8,128)} %occ_hbm.1, bf16[4,8,128,512]{3,2,1,0:T(8,128)(2,1)} %u_hbm.1), custom_call_target="tpu_custom_call" | custom-call | tf_op jit(solution)/shard_map/burst/pallas_call | solution.py:494
  18.2 0.6 %fusion.1 = (f32[32,128]{1,0:T(8,128)}, f32[32,128]{1,0:T(8,128)}) fusion(f32[2,32,128]{2,1,0:T(8,128)S(1)} %burst.1), kind=kLoop, calls=%fused_computation.2 | loop fusion | flops 12288 | bytes 65536 | tf_op jit(solution)/shard_map/add | solution.py:535

commit v4 on v3

--- a/solution.py
+++ b/solution.py
@@ -24,22 +24,6 @@
     gone = 0.6 - 0.6 * jnp.exp2(total)
     kept = x * gone
     return (0.1 * x + kept) + u * (0.6 * SCALE - kept) + 0.075 * total
-
-
-def split_dot(x, onehot):
-    high = x.astype(BF16)
-    low = (x - high.astype(F32)).astype(BF16)
-    return jnp.dot(high, onehot, preferred_element_type=F32) + jnp.dot(
-        low, onehot, preferred_element_type=F32
-    )
-
-
-def split_dot_left(onehot, x):
-    high = x.astype(BF16)
-    low = (x - high.astype(F32)).astype(BF16)
-    return jnp.dot(onehot, high, preferred_element_type=F32) + jnp.dot(
-        onehot, low, preferred_element_type=F32
-    )
 
 
 def kernel(
@@ -101,19 +85,23 @@
         at = (pl.ds(*sweeps), pl.ds(*reals), pl.ds(*rows), pl.ds(*columns))
         load(group, u_hbm.at[at], draws.at[at])
 
-    load_occ("pair0", (0, 2), (0, 128), (0, 512))
-    load_u("pair0", (0, 4), (0, 2), (0, 128), (0, 512))
-    for columns in ((0, 128), (384, 128)):
-        load_occ("edges", (2, 6), (0, 128), columns)
-        load_u("edges", (0, 4), (2, 6), (0, 128), columns)
     for rows in ((0, 16), (112, 16)):
-        load_occ("edges", (2, 6), rows, (128, 256))
-        load_u("edges", (0, 3), (2, 6), rows, (128, 256))
-    for pair in range(1, 4):
-        load_occ("pair%d" % pair, (2 * pair, 2), (16, 96), (128, 256))
-        load_u("pair%d" % pair, (0, 3), (2 * pair, 2), (16, 96), (128, 256))
-        load_u("pair%d" % pair, (3, 1), (2 * pair, 2), (0, 128), (128, 256))
-
+        load_occ("rows", (0, 8), rows, (0, 512))
+        load_u("rows", (0, 3), (0, 8), rows, (0, 512))
+
+    def load_columns():
+        for columns in ((0, 128), (384, 128)):
+            load_occ("columns", (0, 8), (16, 96), columns)
+            load_u("columns", (0, 3), (0, 8), (16, 96), columns)
+
+    def load_rest(pairs):
+        for pair in pairs:
+            load_occ("pair%d" % pair, (2 * pair, 2), (16, 96), (128, 256))
+            load_u("pair%d" % pair, (0, 3), (2 * pair, 2), (16, 96), (128, 256))
+            load_u("pair%d" % pair, (3, 1), (2 * pair, 2), (0, 128), (0, 512))
+
+    load_columns()
+    load_rest((0,))
     barrier = pltpu.get_barrier_semaphore()
     lattice = [
         (gx, left),
@@ -189,23 +177,26 @@
                 totals[t] = value if totals[t] is None else totals[t] + value
         return totals
 
+    def chosen(first, shifted, even, which):
+        return jnp.where(even, first, shifted) if which == 0 else jnp.where(even, shifted, first)
+
     def paired(first, second, even, which):
-        shifted = pltpu.roll(second, 511, 1)
-        return jnp.where(even, first, shifted) if which == 0 else jnp.where(even, shifted, first)
+        return chosen(first, pltpu.roll(second, 511, 1), even, which)
 
     def pack(pair):
         def rows(c, carry):
             at = pl.multiple_of(c * 16, 16)
-            first = occ[2 * pair, pl.ds(at, 16), :].astype(F32) * SCALE
-            second = occ[2 * pair + 1, pl.ds(at, 16), :].astype(F32) * SCALE
+            first = occ[2 * pair, pl.ds(at, 16), :].astype(F32).astype(BF16)
+            second = occ[2 * pair + 1, pl.ds(at, 16), :].astype(F32).astype(BF16)
+            shifted = pltpu.roll(second, 511, 1)
             for which in range(2):
-                both = paired(first, second, wide_even, which)
+                both = chosen(first, shifted, wide_even, which).astype(F32) * SCALE
                 for t in range(4):
                     st[which, pair, t, pl.ds(8 + at, 16), :] = both[:, 128 * t : 128 * t + 128]
             for s in range(4):
-                first = draws[s, 2 * pair, pl.ds(at, 16), :].astype(F32)
-                second = draws[s, 2 * pair + 1, pl.ds(at, 16), :].astype(F32)
-                both = paired(first, second, wide_even, s % 2)
+                first = draws[s, 2 * pair, pl.ds(at, 16), :]
+                second = draws[s, 2 * pair + 1, pl.ds(at, 16), :]
+                both = paired(first, second, wide_even, s % 2).astype(F32)
                 for t in range(4):
                     uu[s, pair, t, pl.ds(at, 16), :] = both[:, 128 * t : 128 * t + 128]
             return carry
@@ -225,19 +216,16 @@
                     st, s, 8 + at, (pair,), lambda p, t: uu[s, p, t, pl.ds(at, 8), :]
                 )
                 for t in range(4):
-                    columns = slice(128 * t, 128 * t + 128)
                     if pair == 0:
-                        sums[s, pl.ds(at, 8), columns] = totals[t]
+                        sums[s, t, pl.ds(at, 8), :] = totals[t]
                     else:
-                        sums[s, pl.ds(at, 8), columns] += totals[t]
+                        sums[s, t, pl.ds(at, 8), :] += totals[t]
                 return carry
 
             lax.fori_loop(0, 16, rows, 0, unroll=16)
 
-    arrived("pair0")
-    pack(0)
-    interior(0)
-    arrived("edges")
+    arrived("rows")
+    load_rest((1, 2, 3))
 
     def edge_columns(real, load_real):
         tiles = []
@@ -247,36 +235,54 @@
             jnp.concatenate(tiles, axis=1), place[real], preferred_element_type=F32
         )
 
-    def put_merged(q, value):
-        merged[q] = value.astype(BF16)
-        return value
-
-    wholes = [edge_columns(r, lambda i, c: occ[i, :, c : c + 128].astype(F32).astype(BF16)) for r in (0, 1)]
-    strips = [
-        put_merged(0, jnp.where(tile_even, wholes[0], wholes[1])),
-        put_merged(1, jnp.where(tile_even, wholes[1], wholes[0])),
-    ]
-    for s in range(4):
-        wholes = [edge_columns(r, lambda i, c: draws[s, i, :, c : c + 128]) for r in (0, 1)]
-        strips.append(
-            put_merged(2 + s, jnp.where(tile_even, wholes[s % 2], wholes[1 - s % 2]))
-        )
-    slot = (iota((128, 128), 1) % 32) // 9
-    sent = (
-        jnp.where(
-            slot == 0,
-            pltpu.roll(strips[0], 117, 1),
-            jnp.where(slot == 1, pltpu.roll(strips[1], 126, 1), pltpu.roll(strips[2], 7, 1)),
-        ),
-        jnp.where(slot == 0, pltpu.roll(strips[3], 117, 1), pltpu.roll(strips[4], 126, 1)),
-    )
-    for part in range(2):
-        side_send[part] = sent[part].astype(BF16)
-        corner_send[0, part] = sent[part][0:8].astype(BF16)
-        corner_send[1, part] = sent[part][120:128].astype(BF16)
-    for q in range(5):
-        vert_send[0, 32 + q] = strips[q][0:8].astype(BF16)
-        vert_send[1, 32 + q] = strips[q][120:128].astype(BF16)
+    def occupied(rows):
+        return [
+            edge_columns(r, lambda i, c: occ[i, rows, c : c + 128].astype(F32).astype(BF16))
+            for r in (0, 1)
+        ]
+
+    def drawn(s, rows):
+        return [edge_columns(r, lambda i, c: draws[s, i, rows, c : c + 128]) for r in (0, 1)]
+
+    def strips_of(rows):
+        even = tile_even[0 : rows.stop - rows.start]
+        real0, real1 = occupied(rows)
+        strips = [jnp.where(even, real0, real1), jnp.where(even, real1, real0)]
+        for s in range(3):
+            pair = drawn(s, rows)
+            strips.append(jnp.where(even, pair[s % 2], pair[1 - s % 2]))
+        return strips
+
+    def squeezed(strips):
+        slot = (iota(strips[0].shape, 1) % 32) // 9
+        return (
+            jnp.where(
+                slot == 0,
+                pltpu.roll(strips[0], 117, 1),
+                jnp.where(slot == 1, pltpu.roll(strips[1], 126, 1), pltpu.roll(strips[2], 7, 1)),
+            ),
+            jnp.where(slot == 0, pltpu.roll(strips[3], 117, 1), pltpu.roll(strips[4], 126, 1)),
+        )
+
+    def send(slot, src, dst, a, b):
+        copy = pltpu.make_async_remote_copy(
+            src_ref=src,
+            dst_ref=dst,
+            send_sem=send_sem.at[slot],
+            recv_sem=recv_sem.at[slot],
+            device_id=(a, b, row),
+            device_id_type=MESH,
+        )
+        copy.start()
+        return copy
+
+    for end in range(2):
+        strips = strips_of(slice(0, 16) if end == 0 else slice(112, 128))
+        keep = slice(0, 8) if end == 0 else slice(8, 16)
+        for part, value in enumerate(squeezed(strips)):
+            corner_send[end, part] = value[keep].astype(BF16)
+        for q in range(5):
+            vert_send[end, 32 + q] = strips[q][keep].astype(BF16)
 
     even8 = wide_even[0:8]
     sub_wide = iota((8, 512), 0)
@@ -311,50 +317,81 @@
                 for t in range(4):
                     vert_send[end, 8 * pair + 2 * t + n] = packed[:, 128 * t : 128 * t + 128]
 
+    arrived("columns")
+    strips = strips_of(slice(0, 128))
+    for q in range(5):
+        merged[q] = strips[q].astype(BF16)
+    for part, value in enumerate(squeezed(strips)):
+        side_send[part] = value.astype(BF16)
     pl.semaphore_wait(barrier, 8 + nrow - 1)
-
-    def send(slot, src, dst, a, b):
-        copy = pltpu.make_async_remote_copy(
-            src_ref=src,
-            dst_ref=dst,
-            send_sem=send_sem.at[slot],
-            recv_sem=recv_sem.at[slot],
-            device_id=(a, b, row),
-            device_id_type=MESH,
-        )
-        copy.start()
-        return copy
-
-    copies = [
+    corner_copies = [
         send(4, corner_send.at[1], corner.at[0], down, right),
         send(5, corner_send.at[1], corner.at[1], down, left),
         send(6, corner_send.at[0], corner.at[2], up, right),
         send(7, corner_send.at[0], corner.at[3], up, left),
+    ]
+
+    row_copies = [
         send(2, vert_send.at[1], vert.at[0], down, gy),
         send(3, vert_send.at[0], vert.at[1], up, gy),
+    ]
+    column_copies = [
         send(0, side_send, side.at[0], gx, right),
         send(1, side_send, side.at[1], gx, left),
     ]
 
-    for pair in range(1, 4):
+    for pair in range(4):
         arrived("pair%d" % pair)
         pack(pair)
         interior(pair)
-
-    coarse_row = iota((32, 128), 0)
-    all_rows = iota((32, 128), 1) // BLOCK == coarse_row
-    rows_all = jnp.where(all_rows, 1.0, 0.0).astype(BF16)
-    rows_inner = jnp.where(all_rows & (coarse_row > 0) & (coarse_row < 31), 1.0, 0.0).astype(BF16)
-    even_wide = ((iota((128, 512), 0) + iota((128, 512), 1)) % 2) == 0
-
+    real0, real1 = drawn(3, slice(0, 128))
+    last_strip = jnp.where(tile_even, real1, real0)
+    ucs[3, 8:136, :] = last_strip
+
+    lane32 = iota((32, 128), 1)
+    row32 = iota((32, 128), 0)
+    inner = (row32 > 0) & (row32 < 31)
+
+    def cell_rows(p_of, q_of):
+        real0, real1 = 0.0, 0.0
+        for k in range(4):
+            even, p, q = (lane32 + k) % 2 == 0, p_of(k), q_of(k)
+            real0 += jnp.where(even, p, q)
+            real1 += jnp.where(even, q, p)
+        return real0, real1
+
+    def halves(x):
+        high = x.astype(BF16).astype(F32)
+        return [high, x - high]
+
+    def dots(pieces, tables):
+        return sum(
+            jnp.dot(
+                jnp.concatenate(pieces[real], axis=0).astype(BF16),
+                tables[real],
+                preferred_element_type=F32,
+            )
+            for real in range(2)
+        )
+
+    pieces = ([], [])
     for which in range(2):
-        p, q = sums[2 * which], sums[2 * which + 1]
-        by_column = split_dot(jnp.where(even_wide, p, q), pick[0]) + split_dot(
-            jnp.where(even_wide, q, p), pick[1]
-        )
-        main_part[which] = split_dot_left(rows_inner, by_column)
-
-    for copy in copies:
+        tiles = ([], [])
+        for t in range(4):
+            both = cell_rows(
+                lambda k: sums[2 * which, t, pl.ds(k, 32, stride=4), :],
+                lambda k: sums[2 * which + 1, t, pl.ds(k, 32, stride=4), :],
+            )
+            for real in range(2):
+                tiles[real].append(jnp.where(inner, both[real], 0.0))
+        for real in range(2):
+            pieces[real].extend(halves(jnp.concatenate(tiles[real], axis=1)))
+    by_cell = dots(pieces, pick)
+    for which in range(2):
+        at = 64 * which
+        main_part[which] = by_cell[at : at + 32] + by_cell[at + 32 : at + 64]
+
+    for copy in row_copies:
         copy.wait()
 
     for pair in range(4):
@@ -368,6 +405,9 @@
             above, below = vert[0, base + 1].astype(F32), vert[1, base + 1].astype(F32)
             rs[0, pair, t, 16:24, :] = jnp.where(low, below, above) * SCALE
             ub[1, pair, t] = pltpu.roll(jnp.where(low, above, below), 4, 0)
+
+    for copy in corner_copies + column_copies:
+        copy.wait()
 
     def strip(q, own, from_left, from_right):
         shape = own.shape
@@ -412,7 +452,6 @@
                     corner[2 * end + 1, n].astype(F32),
                 ),
             )
-    put(5, 8, merged[5].astype(F32))
 
     def share(which):
         out = []
@@ -431,19 +470,26 @@
 
     def edge_part(which):
         p, q = 2 * which, 2 * which + 1
-        even = jnp.concatenate([rsums[p, 1], rsums[p, 0]], axis=0)
-        odd = jnp.concatenate([rsums[q, 1], rsums[q, 0]], axis=0)
-        by_row = split_dot(jnp.where(wide_even, even, odd), pick[0]) + split_dot(
-            jnp.where(wide_even, odd, even), pick[1]
-        )
-        even, odd = cs[0, 16:144, :], cs[1, 16:144, :]
-        by_column = split_dot(jnp.where(tile_even, even, odd), edge_pick[0]) + split_dot(
-            jnp.where(tile_even, odd, even), edge_pick[1]
-        )
-        top = by_column[0:8] + jnp.where(low, by_row[0:8], 0.0)
-        bottom = by_column[120:128] + jnp.where(low, 0.0, by_row[8:16])
-        by_column = jnp.concatenate([top, by_column[8:120], bottom], axis=0)
-        return split_dot_left(rows_all, by_column)
+        both = cell_rows(
+            lambda k: cs[0, pl.ds(16 + k, 32, stride=4), :],
+            lambda k: cs[1, pl.ds(16 + k, 32, stride=4), :],
+        )
+        by_cell = dots([halves(both[0]), halves(both[1])], edge_pick)
+        by_cell = by_cell[0:32] + by_cell[32:64]
+        low_wide = sub_wide < 4
+        p = jnp.where(low_wide, rsums[p, 1], rsums[p, 0])
+        q = jnp.where(low_wide, rsums[q, 1], rsums[q, 0])
+        pieces = []
+        for real in range(2):
+            x = chosen(p, q, even8, real)
+            x = x + pltpu.roll(x, 7, 0)
+            x = x + pltpu.roll(x, 6, 0)
+            pieces.append(halves(x))
+        by_row = dots(pieces, pick)
+        by_row = by_row[0:8] + by_row[8:16]
+        top = by_cell[0:8] + jnp.where(sub == 0, by_row, 0.0)
+        bottom = by_cell[24:32] + jnp.where(sub == 7, pltpu.roll(by_row, 3, 0), 0.0)
+        return jnp.concatenate([top, by_cell[8:24], bottom], axis=0)
 
     shared = []
     for s in range(4):
@@ -502,7 +548,7 @@
                 pltpu.VMEM((4, 8, 128, 512), BF16),
                 pltpu.VMEM((2, 4, 4, 144, 128), F32),
                 pltpu.VMEM((4, 4, 4, 128, 128), F32),
-                pltpu.VMEM((4, 128, 512), F32),
+                pltpu.VMEM((4, 4, 128, 128), F32),
                 pltpu.VMEM((2, 4, 4, 40, 128), F32),
                 pltpu.VMEM((3, 4, 4, 8, 128), F32),
                 pltpu.VMEM((4, 2, 8, 512), F32),
@@ -511,7 +557,7 @@
                 pltpu.VMEM((2, 1024, 128), BF16),
                 pltpu.VMEM((2, 512, 128), BF16),
                 pltpu.VMEM((2, 128, 128), BF16),
-                pltpu.VMEM((6, 128, 128), BF16),
+                pltpu.VMEM((5, 128, 128), BF16),
                 pltpu.VMEM((2, 128, 128), BF16),
                 pltpu.VMEM((2, 2, 128, 128), BF16),
                 pltpu.VMEM((2, 2, 8, 128), BF16),
@@ -521,7 +567,7 @@
                 pltpu.VMEM((2, 32, 128), F32),
                 pltpu.VMEM((2, 32, 128), F32),
                 pltpu.VMEM((nrow - 1, 2, 32, 128), F32),
-                pltpu.SemaphoreType.DMA((19,)),
+                pltpu.SemaphoreType.DMA((20,)),
                 pltpu.SemaphoreType.DMA((8,)),
                 pltpu.SemaphoreType.DMA((8,)),
                 pltpu.SemaphoreType.DMA((2, nrow - 1)),

time: 19 us -> 18.5 us (0.974)
  Pallas kernels: 17.6 us -> 17.1 us
    pallas_call x1, Pallas kernels: 17.6 us -> 17.1 us  [per_device(): pl.pallas_call(functools.partial(kernel, sizes), name='burst', out_shape=...]
where the time goes in v4:
time: 18.5 us; the launch traced here: 18.4 us
  Pallas kernels  17.1 us (92%)
  between operations  0.64 us (3%)
  other arithmetic  0.62 us (3%)
    pallas_call x1, Pallas kernels, per_device(): pl.pallas_call(functools.partial(kernel, sizes), name='burst', out_shape=...  17.1 us
    add x1, other arithmetic, per_device(): return (coverage, coverage + LEAP / 2.0 * (coverage - averages[0]))  0.62 us

profile of v4, /device:TPU:0, one launch (start us, length us, event | category | flops | bytes accessed | tf_op | source)
XLA Modules:
  0.0 18.4 jit_solution(9006692000412958510)
XLA Ops:
  0.6 17.1 %burst.1 = f32[2,32,128]{2,1,0:T(8,128)S(1)} custom-call(s32[8,128,512]{2,1,0:T(8,128)} %occ_hbm.1, bf16[4,8,128,512]{3,2,1,0:T(8,128)(2,1)} %u_hbm.1), custom_call_target="tpu_custom_call" | custom-call | tf_op jit(solution)/shard_map/burst/pallas_call | solution.py:540
  17.8 0.6 %fusion.1 = (f32[32,128]{1,0:T(8,128)}, f32[32,128]{1,0:T(8,128)}) fusion(f32[2,32,128]{2,1,0:T(8,128)S(1)} %burst.1), kind=kLoop, calls=%fused_computation.2 | loop fusion | flops 12288 | bytes 65536 | tf_op jit(solution)/shard_map/add | solution.py:581

commit v5 on v4

--- a/solution.py
+++ b/solution.py
@@ -52,8 +52,9 @@
     vert_send,
     vert,
     main_part,
-    red_send,
-    red,
+    red_main,
+    edge_send,
+    red_edge,
     load_sem,
     send_sem,
     recv_sem,
@@ -193,15 +194,9 @@
                 both = chosen(first, shifted, wide_even, which).astype(F32) * SCALE
                 for t in range(4):
                     st[which, pair, t, pl.ds(8 + at, 16), :] = both[:, 128 * t : 128 * t + 128]
-            for s in range(4):
-                first = draws[s, 2 * pair, pl.ds(at, 16), :]
-                second = draws[s, 2 * pair + 1, pl.ds(at, 16), :]
-                both = paired(first, second, wide_even, s % 2).astype(F32)
-                for t in range(4):
-                    uu[s, pair, t, pl.ds(at, 16), :] = both[:, 128 * t : 128 * t + 128]
             return carry
 
-        lax.fori_loop(0, 8, rows, 0, unroll=4)
+        lax.fori_loop(0, 8, rows, 0, unroll=8)
         for which in range(2):
             for t in range(4):
                 rs[which, pair, t, 8:16, :] = st[which, pair, t, 128:136, :]
@@ -209,20 +204,24 @@
 
     def interior(pair):
         for s in range(4):
-
-            def rows(c, carry, s=s):
-                at = pl.multiple_of(c * 8, 8)
-                totals = update_rows(
-                    st, s, 8 + at, (pair,), lambda p, t: uu[s, p, t, pl.ds(at, 8), :]
-                )
-                for t in range(4):
-                    if pair == 0:
-                        sums[s, t, pl.ds(at, 8), :] = totals[t]
-                    else:
-                        sums[s, t, pl.ds(at, 8), :] += totals[t]
-                return carry
-
-            lax.fori_loop(0, 16, rows, 0, unroll=16)
+            for at in range(0, 128, 16):
+                u = paired(
+                    draws[s, 2 * pair, at : at + 16, :],
+                    draws[s, 2 * pair + 1, at : at + 16, :],
+                    wide_even,
+                    s % 2,
+                ).astype(F32)
+                for half in (0, 8):
+                    here = [u[half : half + 8, 128 * t : 128 * t + 128] for t in range(4)]
+                    if at + half in (0, 120):
+                        for t in range(4):
+                            uu[(at + half) // 120, s, pair, t] = here[t]
+                    totals = update_rows(st, s, 8 + at + half, (pair,), lambda p, t: here[t])
+                    for t in range(4):
+                        if pair == 0:
+                            sums[s, t, pl.ds(at + half, 8), :] = totals[t]
+                        else:
+                            sums[s, t, pl.ds(at + half, 8), :] += totals[t]
 
     arrived("rows")
     load_rest((1, 2, 3))
@@ -391,6 +390,23 @@
         at = 64 * which
         main_part[which] = by_cell[at : at + 32] + by_cell[at + 32 : at + 64]
 
+    def share(stage, src, dst):
+        out = []
+        for d in range(1, nrow):
+            copy = pltpu.make_async_remote_copy(
+                src_ref=src,
+                dst_ref=dst.at[d - 1],
+                send_sem=red_send_sem.at[stage, d - 1],
+                recv_sem=red_recv_sem.at[stage, d - 1],
+                device_id=(gx, gy, peers[d - 1]),
+                device_id_type=MESH,
+            )
+            copy.start()
+            out.append(copy)
+        return out
+
+    shared = share(0, main_part, red_main)
+
     for copy in row_copies:
         copy.wait()
 
@@ -453,20 +469,10 @@
                 ),
             )
 
-    def share(which):
-        out = []
-        for d in range(1, nrow):
-            copy = pltpu.make_async_remote_copy(
-                src_ref=red_send.at[which],
-                dst_ref=red.at[d - 1, which],
-                send_sem=red_send_sem.at[which, d - 1],
-                recv_sem=red_recv_sem.at[which, d - 1],
-                device_id=(gx, gy, peers[d - 1]),
-                device_id_type=MESH,
-            )
-            copy.start()
-            out.append(copy)
-        return out
+    end_lane = (lane32 == 0) | (lane32 == 127)
+
+    def turned(x, amount, dim):
+        return pltpu.roll(x, amount % x.shape[dim], dim) if amount % x.shape[dim] else x
 
     def edge_part(which):
         p, q = 2 * which, 2 * which + 1
@@ -487,20 +493,22 @@
             pieces.append(halves(x))
         by_row = dots(pieces, pick)
         by_row = by_row[0:8] + by_row[8:16]
-        top = by_cell[0:8] + jnp.where(sub == 0, by_row, 0.0)
-        bottom = by_cell[24:32] + jnp.where(sub == 7, pltpu.roll(by_row, 3, 0), 0.0)
-        return jnp.concatenate([top, by_cell[8:24], bottom], axis=0)
-
-    shared = []
+        ends = jnp.where(end_lane, by_cell, 0.0)
+        columns = sum(
+            turned(ends[8 * k : 8 * k + 8], 2 * (4 * which + k), 1) for k in range(4)
+        )
+        return columns, turned(jnp.where((sub == 0) | (sub == 4), by_row, 0.0), which, 0)
+
+    edges = []
     for s in range(4):
         x, y = s % 2, 1 - s % 2
         for part in range(3):
             if s == 3 and part == 1:
                 continue
             u_of = (
-                lambda pair, t: uu[s, pair, t, 120:128, :],
+                lambda pair, t: uu[1, s, pair, t],
                 lambda pair, t: ub[s, pair, t],
-                lambda pair, t: uu[s, pair, t, 0:8, :],
+                lambda pair, t: uu[0, s, pair, t],
             )[part]
             totals = update_rows(rs, s, 8 + 8 * part, range(4), u_of)
             if part != 1:
@@ -518,16 +526,30 @@
                 cs[x, 8 + at : 16 + at, :], total, ucs[s, at : at + 8, :]
             )
         if s % 2 == 1:
-            red_send[s // 2] = main_part[s // 2] + edge_part(s // 2)
-            shared += share(s // 2)
+            edges.append(edge_part(s // 2))
+    for k in range(2):
+        edge_send[k] = edges[0][k] + edges[1][k]
+    shared += share(1, edge_send, red_edge)
 
     for copy in shared:
         copy.wait()
+    columns, rows = edge_send[0], edge_send[1]
+    for d in range(nrow - 1):
+        columns, rows = columns + red_edge[d, 0], rows + red_edge[d, 1]
+    scale = 1.0 / (SCALE * 8 * nrow * BLOCK * BLOCK)
     for which in range(2):
-        total = red_send[which]
-        for d in range(1, nrow):
-            total = total + red[d - 1, which]
-        average_ref[which] = total * (1.0 / (SCALE * 8 * nrow * BLOCK * BLOCK))
+        total = main_part[which]
+        for d in range(nrow - 1):
+            total = total + red_main[d, which]
+        for k in range(4):
+            part = total[8 * k : 8 * k + 8] + jnp.where(
+                end_lane[0:8], turned(columns, -2 * (4 * which + k), 1), 0.0
+            )
+            if k == 0:
+                part = part + jnp.where(sub == 0, turned(rows, -which, 0), 0.0)
+            if k == 3:
+                part = part + jnp.where(sub == 7, turned(rows, 3 - which, 0), 0.0)
+            average_ref[which, 8 * k : 8 * k + 8, :] = part * scale
 
 
 def solution(mesh):
@@ -547,7 +569,7 @@
                 pltpu.VMEM((8, 128, 512), jnp.int32),
                 pltpu.VMEM((4, 8, 128, 512), BF16),
                 pltpu.VMEM((2, 4, 4, 144, 128), F32),
-                pltpu.VMEM((4, 4, 4, 128, 128), F32),
+                pltpu.VMEM((2, 4, 4, 4, 8, 128), F32),
                 pltpu.VMEM((4, 4, 128, 128), F32),
                 pltpu.VMEM((2, 4, 4, 40, 128), F32),
                 pltpu.VMEM((3, 4, 4, 8, 128), F32),
@@ -565,8 +587,9 @@
                 pltpu.VMEM((2, 37, 8, 128), BF16),
                 pltpu.VMEM((2, 37, 8, 128), BF16),
                 pltpu.VMEM((2, 32, 128), F32),
-                pltpu.VMEM((2, 32, 128), F32),
                 pltpu.VMEM((nrow - 1, 2, 32, 128), F32),
+                pltpu.VMEM((2, 8, 128), F32),
+                pltpu.VMEM((nrow - 1, 2, 8, 128), F32),
                 pltpu.SemaphoreType.DMA((20,)),
                 pltpu.SemaphoreType.DMA((8,)),
                 pltpu.SemaphoreType.DMA((8,)),

time: 18.5 us -> 17.9 us (0.968)
  Pallas kernels: 17.1 us -> 16.5 us
    pallas_call x1, Pallas kernels: 17.1 us -> 16.5 us  [per_device(): pl.pallas_call(functools.partial(kernel, sizes), name='burst', out_shape=...]
where the time goes in v5:
time: 17.9 us; the launch traced here: 17.8 us
  Pallas kernels  16.5 us (92%)
  between operations  0.64 us (4%)
  other arithmetic  0.62 us (3%)
    pallas_call x1, Pallas kernels, per_device(): pl.pallas_call(functools.partial(kernel, sizes), name='burst', out_shape=...  16.5 us
    add x1, other arithmetic, per_device(): return (coverage, coverage + LEAP / 2.0 * (coverage - averages[0]))  0.62 us

profile of v5, /device:TPU:0, one launch (start us, length us, event | category | flops | bytes accessed | tf_op | source)
XLA Modules:
  0.0 17.8 jit_solution(1817539189427611029)
XLA Ops:
  0.6 16.5 %burst.1 = f32[2,32,128]{2,1,0:T(8,128)S(1)} custom-call(s32[8,128,512]{2,1,0:T(8,128)} %occ_hbm.1, bf16[4,8,128,512]{3,2,1,0:T(8,128)(2,1)} %u_hbm.1), custom_call_target="tpu_custom_call" | custom-call | tf_op jit(solution)/shard_map/burst/pallas_call | solution.py:562
  17.2 0.6 %fusion.1 = (f32[32,128]{1,0:T(8,128)}, f32[32,128]{1,0:T(8,128)}) fusion(f32[2,32,128]{2,1,0:T(8,128)S(1)} %burst.1), kind=kLoop, calls=%fused_computation.2 | loop fusion | flops 12288 | bytes 65536 | tf_op jit(solution)/shard_map/add | solution.py:604
